TPU v7x, 32 devices: a whole 2x2x4 slice. The times are simulated.
32 devices in a mesh: gx: 8 (over z, y), gy: 4 (over x, core).
Axes of the slice: x: 2, y: 2, z: 4, core: 2. Of those that a mesh axis runs over, the one named last changes fastest.
Arguments:
- features: bfloat16 [8, 4, 2048, 256], P('gx', 'gy'), may hold values from -6 to 6
- pre_norm: bfloat16 [8, 4, 2048, 256], P('gx', 'gy')
- out_grad: bfloat16 [8, 4, 2048, 256], P('gx', 'gy'), may hold values from -6 to 6
- weight: bfloat16 [27, 256, 256], replicated, may hold values from -0.375 to 0.375
- gamma: float32 [256], replicated, may hold values from 0.1 to 1.9
- beta: float32 [256], replicated, may hold values from -3 to 3
- neighbors: int32 [8, 4, 27, 2048], P('gx', 'gy'), may hold values from 0 to 8384, as said below
- boundary: int32 [8, 4, 704], P('gx', 'gy'), may hold values from 0 to 2048, as said below
- counts: int32 [8, 4], P('gx', 'gy'), may hold values from 1 to 2048, as said below
Outputs:
- in_grad: bfloat16 [8, 4, 2048, 256], P('gx', 'gy')
- weight_grad: float32 [6912, 256], P(('gx', 'gy'))
- gamma_grad: float32 [256], replicated
- beta_grad: float32 [256], replicated
Inputs may be any that keep to these rules, and one draw needn't show every extreme that they name: `neighbors`: the map is that of a submanifold convolution on a voxel grid: each device owns an 8 x 16 x 16 block of positions, its live rows are its occupied positions in order, rows at or past its count name no row at any offset, offset 13 names the row itself, and if pair (r, k) on one device names row q then row q's device names r at offset 26 - k. Rows named on other devices lie on that device's faces and are listed in its boundary list. `boundary`: A device's live rows on its x and y faces in increasing order, then 2048 in the unused slots. `counts`: some device holds 2048 live rows.
All inputs are finite; a program needn't handle non-finite values.
Results may differ from a plain program's by a relative error of at most 0.0049.
Values may be sent and summed in bfloat16 or wider, within the bound.
No kernel may reach another device: no remote copies, remote signals or barrier semaphores. Data moves between devices by JAX's collectives and lax.ppermute only.
A program may use at most 64 MiB of HBM per device.

v0:
```python
import jax
import jax.numpy as jnp
from jax import lax
from jax.sharding import PartitionSpec as P


def extended(block, sides, width):
    for axis, dim in sides:
        count = lax.axis_size(axis)
        forward = [(i, i + 1) for i in range(count - 1)]
        backward = [(target, source) for source, target in forward]
        low = lax.ppermute(
            lax.slice_in_dim(block, block.shape[dim] - width, None, axis=dim), axis, forward
        )
        high = lax.ppermute(lax.slice_in_dim(block, 0, width, axis=dim), axis, backward)
        block = jnp.concatenate([low, block, high], axis=dim)
    return block


def gather_rows(local, border):
    padded = jnp.concatenate([local, jnp.zeros((1, local.shape[1]), local.dtype)], axis=0)
    return jnp.take(padded, border, axis=0, mode="clip")


def make_table(local, around):
    flat = around.reshape(-1, local.shape[1])
    return jnp.concatenate([local, flat, jnp.zeros((1, local.shape[1]), local.dtype)], axis=0)


def body(features, pre_norm, out_grad, weight, gamma, beta, neighbors, boundary, counts):
    feat = features[0, 0]
    rows = feat.shape[0]
    chans = feat.shape[1]
    border = boundary[0, 0]
    links = neighbors[0, 0]
    live = (lax.iota(jnp.int32, rows) < counts[0, 0])[:, None]
    zval = pre_norm[0, 0].astype(jnp.float32)
    zlive = jnp.where(live, zval, jnp.float32(0.0))
    sum_z, sum_sq, sum_count = lax.psum(
        (jnp.sum(zlive, axis=0), jnp.sum(zlive * zval, axis=0), counts[0].astype(jnp.float32)),
        ("gx", "gy"),
    )
    count = sum_count[0]
    mean = sum_z / count
    var = sum_sq / count - mean * mean
    rstd = lax.rsqrt(var + 1e-05)
    zhat = (zval - mean) * rstd
    act = gamma * zhat + beta
    sig = jax.nn.sigmoid(act)
    grad_act = jnp.where(
        live, out_grad[0, 0].astype(jnp.float32) * sig * (1.0 + act * (1.0 - sig)), jnp.float32(0.0)
    )
    beta_grad, gamma_grad = lax.psum(
        (jnp.sum(grad_act, axis=0), jnp.sum(grad_act * zhat, axis=0)), ("gx", "gy")
    )
    dz = jnp.where(
        live,
        gamma * rstd * (grad_act - beta_grad / count - zhat * gamma_grad / count),
        jnp.float32(0.0),
    ).astype(jnp.bfloat16)
    grad_edge = gather_rows(dz, border)
    grad_around = extended(grad_edge[None, None], (("gx", 0), ("gy", 1)), 1)
    grad_table = make_table(dz, grad_around)

    def offset_step(accum, item):
        mirror_row, w_k = item
        picked = jnp.take(grad_table, mirror_row, axis=0, mode="clip")
        accum = accum + lax.dot_general(
            picked, w_k, (((1,), (1,)), ((), ())), preferred_element_type=jnp.float32
        )
        term = lax.dot_general(
            feat, picked, (((0,), (0,)), ((), ())), preferred_element_type=jnp.float32
        )
        return (accum, term)

    in_accum, wterms = lax.scan(
        offset_step, jnp.zeros((rows, chans), jnp.float32), (links[::-1], weight)
    )
    local_wgrad = wterms.reshape(-1, chans)
    weight_grad = lax.psum_scatter(local_wgrad, ("gx", "gy"), scatter_dimension=0, tiled=True)
    in_grad = in_accum.astype(jnp.bfloat16)[None, None]
    return (in_grad, weight_grad, gamma_grad, beta_grad)


def solution(mesh):
    placed = (
        P("gx", "gy", None, None),
        P("gx", "gy", None, None),
        P("gx", "gy", None, None),
        P(),
        P(),
        P(),
        P("gx", "gy", None, None),
        P("gx", "gy", None),
        P("gx", "gy"),
    )
    return jax.shard_map(
        body,
        mesh=mesh,
        in_specs=placed,
        out_specs=(P("gx", "gy", None, None), P(("gx", "gy"), None), P(), P()),
        check_vma=False,
    )
```

profile of v0, /device:TPU:0, one launch (start us, length us, event | category | flops | bytes accessed | tf_op | source)
XLA Modules:
  0.0 695.9 jit_solution(10537505351151717233)
XLA Ops:
  10.2 42.7 %all-reduce.2 = (f32[256]{0:T(256)S(1)}, f32[]{:T(128)}, f32[256]{0:T(256)S(1)}) all-reduce(f32[256]{0:T(256)S(1)} %get-tuple-element.71, f32[]{:T(128)} %bitcast.2, f32[256]{0:T(256)S(1)} %get-tuple-element.70), channel_id=1, replica_groups=mesh['gx'=8,'gy'=4] {'gx','gy'}, use_global_device_ids=true, to_apply=%region_4.5 | all-reduce | flops 513 | bytes 4104 | tf_op jit(solution)/shard_map/psum | solution.py:39
  58.0 40.2 %all-reduce.1 = (f32[256]{0:T(256)S(1)}, f32[256]{0:T(256)S(1)}) all-reduce(f32[256]{0:T(256)S(1)} %get-tuple-element.69, f32[256]{0:T(256)S(1)} %get-tuple-element.68), channel_id=1, replica_groups=mesh['gx'=8,'gy'=4] {'gx','gy'}, use_global_device_ids=true, to_apply=%region_8.9 | all-reduce | flops 512 | bytes 4096 | tf_op jit(solution)/shard_map/psum | solution.py:53
  142.3 11.1 %maximum_maximum_fusion = bf16[8385,256]{1,0:T(8,128)(2,1)} fusion(bf16[6336,256]{1,0:T(8,128)(2,1)S(1)} %bitcast.49, bf16[2048,256]{1,0:T(8,128)(2,1)S(1)} %fusion.23, bf16[8385]{0:T(1024)(128)(2,1)S(1)} %pad.3.clone), kind=kLoop, calls=%fused_computation.10 | loop fusion | flops 12879360 | bytes 8602498 | tf_op jit(solution)/shard_map/concatenate | solution.py:27
  153.4 412.4 %while.13 = (s32[]{:T(128)}, f32[2048,256]{1,0:T(8,128)S(1)}, f32[27,256,256]{2,1,0:T(8,128)}, s32[27,2048]{1,0:T(8,128)}, bf16[8385,256]{1,0:T(8,128)(2,1)}, /*...) while((s32[]{:T(128)}, f32[2048,256]{1,0:T(8,128)S(1)}, ...), condition=%wide.region_10.11_spmd.clone, body=%wide.region_9.10_spmd.clone.sunk | while | flops 537921536 | bytes 11968663 | solution.py:76
  154.3 9.4 %gather_fusion = bf16[2048,256]{1,0:T(8,128)(2,1)S(1)} fusion(bf16[8385,256]{1,0:T(8,128)(2,1)} %get-tuple-element.160, s32[2048]{0:T(1024)S(1)} %broadcast_clamp_fusion.2), kind=kCustom, calls=%fused_computation.clone.clone.1 | custom fusion | bytes 2105344 | tf_op jit(solution)/shard_map/while/body/eval_jaxpr/jit(_take)/gather | solution.py:67
  169.5 9.4 %gather_fusion = bf16[2048,256]{1,0:T(8,128)(2,1)S(1)} fusion(bf16[8385,256]{1,0:T(8,128)(2,1)} %get-tuple-element.160, s32[2048]{0:T(1024)S(1)} %broadcast_clamp_fusion.2), kind=kCustom, calls=%fused_computation.clone.clone.1 | custom fusion | bytes 2105344 | tf_op jit(solution)/shard_map/while/body/eval_jaxpr/jit(_take)/gather | solution.py:67
  184.8 9.4 %gather_fusion = bf16[2048,256]{1,0:T(8,128)(2,1)S(1)} fusion(bf16[8385,256]{1,0:T(8,128)(2,1)} %get-tuple-element.160, s32[2048]{0:T(1024)S(1)} %broadcast_clamp_fusion.2), kind=kCustom, calls=%fused_computation.clone.clone.1 | custom fusion | bytes 2105344 | tf_op jit(solution)/shard_map/while/body/eval_jaxpr/jit(_take)/gather | solution.py:67
  200.0 9.4 %gather_fusion = bf16[2048,256]{1,0:T(8,128)(2,1)S(1)} fusion(bf16[8385,256]{1,0:T(8,128)(2,1)} %get-tuple-element.160, s32[2048]{0:T(1024)S(1)} %broadcast_clamp_fusion.2), kind=kCustom, calls=%fused_computation.clone.clone.1 | custom fusion | bytes 2105344 | tf_op jit(solution)/shard_map/while/body/eval_jaxpr/jit(_take)/gather | solution.py:67
  215.3 9.4 %gather_fusion = bf16[2048,256]{1,0:T(8,128)(2,1)S(1)} fusion(bf16[8385,256]{1,0:T(8,128)(2,1)} %get-tuple-element.160, s32[2048]{0:T(1024)S(1)} %broadcast_clamp_fusion.2), kind=kCustom, calls=%fused_computation.clone.clone.1 | custom fusion | bytes 2105344 | tf_op jit(solution)/shard_map/while/body/eval_jaxpr/jit(_take)/gather | solution.py:67
  230.6 9.4 %gather_fusion = bf16[2048,256]{1,0:T(8,128)(2,1)S(1)} fusion(bf16[8385,256]{1,0:T(8,128)(2,1)} %get-tuple-element.160, s32[2048]{0:T(1024)S(1)} %broadcast_clamp_fusion.2), kind=kCustom, calls=%fused_computation.clone.clone.1 | custom fusion | bytes 2105344 | tf_op jit(solution)/shard_map/while/body/eval_jaxpr/jit(_take)/gather | solution.py:67
  245.9 9.4 %gather_fusion = bf16[2048,256]{1,0:T(8,128)(2,1)S(1)} fusion(bf16[8385,256]{1,0:T(8,128)(2,1)} %get-tuple-element.160, s32[2048]{0:T(1024)S(1)} %broadcast_clamp_fusion.2), kind=kCustom, calls=%fused_computation.clone.clone.1 | custom fusion | bytes 2105344 | tf_op jit(solution)/shard_map/while/body/eval_jaxpr/jit(_take)/gather | solution.py:67
  261.2 9.4 %gather_fusion = bf16[2048,256]{1,0:T(8,128)(2,1)S(1)} fusion(bf16[8385,256]{1,0:T(8,128)(2,1)} %get-tuple-element.160, s32[2048]{0:T(1024)S(1)} %broadcast_clamp_fusion.2), kind=kCustom, calls=%fused_computation.clone.clone.1 | custom fusion | bytes 2105344 | tf_op jit(solution)/shard_map/while/body/eval_jaxpr/jit(_take)/gather | solution.py:67
  276.4 9.4 %gather_fusion = bf16[2048,256]{1,0:T(8,128)(2,1)S(1)} fusion(bf16[8385,256]{1,0:T(8,128)(2,1)} %get-tuple-element.160, s32[2048]{0:T(1024)S(1)} %broadcast_clamp_fusion.2), kind=kCustom, calls=%fused_computation.clone.clone.1 | custom fusion | bytes 2105344 | tf_op jit(solution)/shard_map/while/body/eval_jaxpr/jit(_take)/gather | solution.py:67
  291.7 9.4 %gather_fusion = bf16[2048,256]{1,0:T(8,128)(2,1)S(1)} fusion(bf16[8385,256]{1,0:T(8,128)(2,1)} %get-tuple-element.160, s32[2048]{0:T(1024)S(1)} %broadcast_clamp_fusion.2), kind=kCustom, calls=%fused_computation.clone.clone.1 | custom fusion | bytes 2105344 | tf_op jit(solution)/shard_map/while/body/eval_jaxpr/jit(_take)/gather | solution.py:67
  307.0 9.4 %gather_fusion = bf16[2048,256]{1,0:T(8,128)(2,1)S(1)} fusion(bf16[8385,256]{1,0:T(8,128)(2,1)} %get-tuple-element.160, s32[2048]{0:T(1024)S(1)} %broadcast_clamp_fusion.2), kind=kCustom, calls=%fused_computation.clone.clone.1 | custom fusion | bytes 2105344 | tf_op jit(solution)/shard_map/while/body/eval_jaxpr/jit(_take)/gather | solution.py:67
  337.6 9.4 %gather_fusion = bf16[2048,256]{1,0:T(8,128)(2,1)S(1)} fusion(bf16[8385,256]{1,0:T(8,128)(2,1)} %get-tuple-element.160, s32[2048]{0:T(1024)S(1)} %broadcast_clamp_fusion.2), kind=kCustom, calls=%fused_computation.clone.clone.1 | custom fusion | bytes 2105344 | tf_op jit(solution)/shard_map/while/body/eval_jaxpr/jit(_take)/gather | solution.py:67
  352.8 9.4 %gather_fusion = bf16[2048,256]{1,0:T(8,128)(2,1)S(1)} fusion(bf16[8385,256]{1,0:T(8,128)(2,1)} %get-tuple-element.160, s32[2048]{0:T(1024)S(1)} %broadcast_clamp_fusion.2), kind=kCustom, calls=%fused_computation.clone.clone.1 | custom fusion | bytes 2105344 | tf_op jit(solution)/shard_map/while/body/eval_jaxpr/jit(_take)/gather | solution.py:67
  368.1 9.4 %gather_fusion = bf16[2048,256]{1,0:T(8,128)(2,1)S(1)} fusion(bf16[8385,256]{1,0:T(8,128)(2,1)} %get-tuple-element.160, s32[2048]{0:T(1024)S(1)} %broadcast_clamp_fusion.2), kind=kCustom, calls=%fused_computation.clone.clone.1 | custom fusion | bytes 2105344 | tf_op jit(solution)/shard_map/while/body/eval_jaxpr/jit(_take)/gather | solution.py:67
  383.4 9.4 %gather_fusion = bf16[2048,256]{1,0:T(8,128)(2,1)S(1)} fusion(bf16[8385,256]{1,0:T(8,128)(2,1)} %get-tuple-element.160, s32[2048]{0:T(1024)S(1)} %broadcast_clamp_fusion.2), kind=kCustom, calls=%fused_computation.clone.clone.1 | custom fusion | bytes 2105344 | tf_op jit(solution)/shard_map/while/body/eval_jaxpr/jit(_take)/gather | solution.py:67
  398.6 9.4 %gather_fusion = bf16[2048,256]{1,0:T(8,128)(2,1)S(1)} fusion(bf16[8385,256]{1,0:T(8,128)(2,1)} %get-tuple-element.160, s32[2048]{0:T(1024)S(1)} %broadcast_clamp_fusion.2), kind=kCustom, calls=%fused_computation.clone.clone.1 | custom fusion | bytes 2105344 | tf_op jit(solution)/shard_map/while/body/eval_jaxpr/jit(_take)/gather | solution.py:67
  413.9 9.4 %gather_fusion = bf16[2048,256]{1,0:T(8,128)(2,1)S(1)} fusion(bf16[8385,256]{1,0:T(8,128)(2,1)} %get-tuple-element.160, s32[2048]{0:T(1024)S(1)} %broadcast_clamp_fusion.2), kind=kCustom, calls=%fused_computation.clone.clone.1 | custom fusion | bytes 2105344 | tf_op jit(solution)/shard_map/while/body/eval_jaxpr/jit(_take)/gather | solution.py:67
  429.2 9.4 %gather_fusion = bf16[2048,256]{1,0:T(8,128)(2,1)S(1)} fusion(bf16[8385,256]{1,0:T(8,128)(2,1)} %get-tuple-element.160, s32[2048]{0:T(1024)S(1)} %broadcast_clamp_fusion.2), kind=kCustom, calls=%fused_computation.clone.clone.1 | custom fusion | bytes 2105344 | tf_op jit(solution)/shard_map/while/body/eval_jaxpr/jit(_take)/gather | solution.py:67
  444.4 9.4 %gather_fusion = bf16[2048,256]{1,0:T(8,128)(2,1)S(1)} fusion(bf16[8385,256]{1,0:T(8,128)(2,1)} %get-tuple-element.160, s32[2048]{0:T(1024)S(1)} %broadcast_clamp_fusion.2), kind=kCustom, calls=%fused_computation.clone.clone.1 | custom fusion | bytes 2105344 | tf_op jit(solution)/shard_map/while/body/eval_jaxpr/jit(_take)/gather | solution.py:67
  566.9 122.1 %reduce-scatter.2.cloned.1.call-done = f32[216,256]{1,0:T(8,128)} async-done(((f32[6912,256]{1,0:T(8,128)}), f32[216,256]{1,0:T(8,128)}) %reduce-scatter.2.cloned.1.call-update) | async-done | bytes 221200 | tf_op jit(solution)/shard_map/reduce_scatter | solution.py:80
  (262 shorter events, 285.3 us)
Async XLA Ops:
  7.2 681.9 %reduce-scatter.2.cloned.1.call-start = ((), (), s32[]{:S(2)}) async-start(), calls=%async_computation.1 | async-start | bytes 7299072 | tf_op jit(solution)/shard_map/reduce_scatter | solution.py:80
  54.3 44.6 %copy-start.1 = (bf16[1,1,2048,256]{3,2,1,0:T(8,128)(2,1)S(1)}, bf16[1,1,2048,256]{3,2,1,0:T(8,128)(2,1)}, u32[]{:S(2)}) copy-start(bf16[1,1,2048,256]{3,2,1,0:T(8,128)(2,1)} %param.12) | copy-start | bytes 3145732
  98.2 3.3 copy-start.4
  98.2 3.3 copy-start.5
  104.4 11.7 %collective-permute-start.1 = (bf16[1,1,704,256]{3,2,1,0:T(8,128)(2,1)S(1)}, bf16[1,1,704,256]{3,2,1,0:T(8,128)(2,1)S(1)}, u32[]{:S(2)}, u32[]{:S(2)}) collective-permute-start(bf16[1,1,704,256]{3,2,1,0:T(8,128)(2,1)S(1)} %bitcast.51), channel_id=1, source_target_pairs={{4,0},{8,4},{12,8},{16,12},{20,16},{24,20},{28,24},{5,1},{9,5},{13... | collective-permute-start | bytes 1081352 | tf_op jit(solution)/shard_map/ppermute | solution.py:15
  105.7 18.3 %collective-permute-start = (bf16[1,1,704,256]{3,2,1,0:T(8,128)(2,1)S(1)}, bf16[1,1,704,256]{3,2,1,0:T(8,128)(2,1)S(1)}, u32[]{:S(2)}, u32[]{:S(2)}) collective-permute-start(bf16[1,1,704,256]{3,2,1,0:T(8,128)(2,1)S(1)} %bitcast.52), channel_id=1, source_target_pairs={{0,4},{4,8},{8,12},{12,16},{16,20},{20,24},{24,28},{1,5},{5,9},{9,... | collective-permute-start | bytes 1081352 | tf_op jit(solution)/shard_map/ppermute | solution.py:12
  116.1 7.9 %copy-start.2 = (bf16[1,1,704,256]{3,2,1,0:T(8,128)(2,1)}, bf16[1,1,704,256]{3,2,1,0:T(8,128)(2,1)S(1)}, u32[]{:S(2)}) copy-start(bf16[1,1,704,256]{3,2,1,0:T(8,128)(2,1)S(1)} %collective-permute-done.1) | copy-start | bytes 1081348
  125.2 15.2 %collective-permute-start.3 = (bf16[3,1,704,256]{3,2,1,0:T(8,128)(2,1)}, bf16[3,1,704,256]{3,2,1,0:T(8,128)(2,1)}, u32[]{:S(2)}, u32[]{:S(2)}) collective-permute-start(bf16[3,1,704,256]{3,2,1,0:T(8,128)(2,1)} %pad_maximum_fusion.1), channel_id=1, source_target_pairs={{1,0},{2,1},{3,2},{5,4},{6,5},{7,6},{9,8},{10,9},{11,10},{13,12},{... | collective-permute-start | bytes 3244040 | tf_op jit(solution)/shard_map/ppermute | solution.py:15
  126.4 13.9 %collective-permute-start.2 = (bf16[3,1,704,256]{3,2,1,0:T(8,128)(2,1)}, bf16[3,1,704,256]{3,2,1,0:T(8,128)(2,1)}, u32[]{:S(2)}, u32[]{:S(2)}) collective-permute-start(bf16[3,1,704,256]{3,2,1,0:T(8,128)(2,1)} %pad_maximum_fusion.1), channel_id=1, source_target_pairs={{0,1},{1,2},{2,3},{4,5},{5,6},{6,7},{8,9},{9,10},{10,11},{12,13},{... | collective-permute-start | bytes 3244040 | tf_op jit(solution)/shard_map/ppermute | solution.py:12
  166.2 1.7 copy-start
  181.5 1.7 copy-start
  227.3 1.7 copy-start
  242.6 1.7 copy-start
  257.8 1.7 copy-start
  303.7 1.7 copy-start
  318.9 1.7 copy-start
  334.2 1.7 copy-start
  380.1 1.7 copy-start
  410.6 1.7 copy-start
  425.8 1.7 copy-start
  456.4 1.7 copy-start
  471.7 1.7 copy-start
  502.2 1.7 copy-start
  548.1 1.7 copy-start
  (13 other events, 21.8 us)
Sparse Core Ops, SparseCore 0:
  565.9 123.0 reduce-scatter.1
where the time goes:
time: 701 us; the launch traced here: 696 us
  local copies, waits for them, and re-layouts  332 us (47%)
  waiting for transfers between devices  136 us (19%)
  matrix products  92.1 us (13%)
  blocking collectives  82.9 us (12%)
  other arithmetic  26.1 us (4%)
  between operations  14.8 us (2%)
  starting transfers between devices  11.6 us (2%)
    gather x27, local copies, waits for them, and re-layouts, offset_step(): picked = jnp.take(grad_table, mirror_row, axis=0, mode='clip')  254 us
    reduce_scatter x1, waiting for transfers between devices, body(): lax.psum_scatter(local_wgrad, ('gx', 'gy'), scatter_dimension=0, tiled=True)  122 us
    dot_general x27, matrix products, offset_step(): lax.dot_general(picked, w_k, (((1,), (1,)), ((), ())), preferred_element_...  46.3 us
    dot_general x27, matrix products, offset_step(): lax.dot_general(feat, picked, (((0,), (0,)), ((), ())), preferred_element...  45.8 us
    psum x1, blocking collectives, body(): lax.psum((jnp.sum(zlive, axis=0), jnp.sum(zlive * zval, axis=0), counts[0...  42.7 us
    dynamic_update_slice x54, local copies, waits for them, and re-layouts, body(): lax.scan(offset_step, jnp.zeros((rows, chans), jnp.float32), (links[::-1]...  42.3 us
    psum x1, blocking collectives, body(): lax.psum((jnp.sum(grad_act, axis=0), jnp.sum(grad_act * zhat, axis=0)), (...  40.2 us
    dynamic_slice x27, local copies, waits for them, and re-layouts, body(): lax.scan(offset_step, jnp.zeros((rows, chans), jnp.float32), (links[::-1]...  22.9 us
  transfers between devices with their start and end apart: 5, of which 3 were waited for; matrix products, arithmetic and copies ran while one was open for 2% of the time, Pallas kernels for 0%

commit v1 on v0

v1 whole, which is shorter than its diff:
```python
import functools

import jax
import jax.numpy as jnp
from jax import lax
from jax.experimental import pallas as pl
from jax.experimental.pallas import tpu as pltpu
from jax.sharding import PartitionSpec as P

TILE = 192
SEG = 16
LANES = 128
SEGS = 16
NOWHERE = -(1 << 20)
LISTED = 3
BF = jnp.bfloat16
F32 = jnp.float32
AXES = ("gx", "gy")


def everyone_sum(vec):
    count = lax.axis_size(AXES)
    spread = jnp.broadcast_to(vec[None], (count,) + vec.shape)
    return jnp.sum(lax.all_to_all(spread, AXES, 0, 0, tiled=True), axis=0)


def shift(block, axis):
    count = lax.axis_size(axis)
    forward = [(i, i + 1) for i in range(count - 1)]
    backward = [(target, source) for source, target in forward]
    return lax.ppermute(block, axis, forward), lax.ppermute(block, axis, backward)


def halve(arr, dim, axis, bit):
    count = lax.axis_size(axis)
    mine = (lax.axis_index(axis) >> bit) & 1
    give = lax.dynamic_index_in_dim(arr, 1 - mine, dim, keepdims=False).astype(BF)
    got = lax.ppermute(give, axis, [(i, i ^ (1 << bit)) for i in range(count)])
    keep = lax.dynamic_index_in_dim(arr, mine, dim, keepdims=False)
    return keep + got.astype(F32)


def scatter_sum(full):
    size_x, size_y = lax.axis_size("gx"), lax.axis_size("gy")
    rows, chans = full.shape
    bits_x, bits_y = size_x.bit_length() - 1, size_y.bit_length() - 1
    part = rows // (size_x * size_y)
    if (1 << bits_x) != size_x or (1 << bits_y) != size_y or bits_x < 1 or bits_y < 2:
        return lax.psum_scatter(full, AXES, scatter_dimension=0, tiled=True)
    arr = full.reshape((2,) * (bits_x + bits_y) + (part, chans))
    order = [("gx", b) for b in reversed(range(bits_x))] + [
        ("gy", b) for b in reversed(range(bits_y))
    ]

    def step(arr, order, which):
        dim = order.index(which)
        return halve(arr, dim, *which), order[:dim] + order[dim + 1 :]

    arr, order = step(arr, order, ("gy", 0))
    pair = [("gy", 1), ("gx", 0)]
    rest = [("gy", b) for b in range(2, bits_y)] + [("gx", b) for b in range(1, bits_x)]
    half = chans // 2
    colours = [(arr[..., :half], order), (arr[..., half:], order)]
    plans = [pair + rest, pair[::-1] + rest]
    for at in range(len(plans[0])):
        colours = [step(a, o, plan[at]) for (a, o), plan in zip(colours, plans)]
    return jnp.concatenate([a for a, _ in colours], axis=-1)


def plan_segments(links, rows, width, tiles):
    offsets = links.shape[0]
    total = rows + 9 * width
    groups = offsets // 3
    named = links < total
    clean = jnp.where(named, links, NOWHERE)
    clean = jnp.pad(clean, ((0, 0), (0, tiles * TILE - rows)), constant_values=NOWHERE)
    laid = clean.reshape(offsets, tiles, TILE).transpose(1, 0, 2)
    laid = jnp.pad(laid, ((0, 0), (0, -offsets % 8), (0, 0)), constant_values=NOWHERE)
    view = clean.reshape(groups, 3, tiles, TILE)
    low_ids, sizes = [], []
    for block in range(10):
        first = 0 if block == 0 else rows + (block - 1) * width
        last = rows if block == 0 else first + width
        inside = (view >= first) & (view < last)
        low = jnp.min(jnp.where(inside, view, total), axis=(1, 3)) // SEG
        high = jnp.max(jnp.where(inside, view, -1), axis=(1, 3))
        low_ids.append(low)
        sizes.append(jnp.where(high >= 0, high // SEG - low + 1, 0))
    low_ids = jnp.stack(low_ids, axis=-1).transpose(1, 0, 2).reshape(tiles * groups, 10)
    sizes = jnp.stack(sizes, axis=-1).transpose(1, 0, 2).reshape(tiles * groups, 10)
    ends = jnp.cumsum(sizes, axis=-1)
    starts = ends - sizes
    passes = (ends[:, -1] + SEGS - 1) // SEGS
    most = -(-(total // SEG) // SEGS)
    slot = lax.iota(jnp.int32, most * SEGS)[None, :, None]
    hit = (slot >= starts[:, None, :]) & (slot < ends[:, None, :])
    listed = jnp.sum(
        jnp.where(hit, low_ids[:, None, :] + slot - starts[:, None, :] + 1, 0), axis=-1
    ) - 1
    return laid, listed.reshape(tiles * groups, most, SEGS), passes


def conv_kernel(
    rows,
    width,
    seg_ref,
    pass_ref,
    all_segs,
    links_ref,
    dz_ref,
    mid_ref,
    low_ref,
    high_ref,
    feat_ref,
    w_ref,
    in_ref,
    wg_ref,
    table,
    cols,
    feat_t,
    acc,
    picked,
    spill,
    sems,
    spill_sem,
):
    tiles = links_ref.shape[0]
    offsets = w_ref.shape[0]
    groups = offsets // 3
    chans = feat_ref.shape[1]
    copies = [pltpu.make_async_copy(dz_ref, table.at[pl.ds(0, rows)], sems.at[0])]
    for da in range(3):
        for db, piece in enumerate((low_ref, mid_ref, high_ref)):
            copies.append(
                pltpu.make_async_copy(
                    piece.at[da],
                    table.at[pl.ds(rows + (3 * da + db) * width, width)],
                    sems.at[1 + 3 * da + db],
                )
            )
    for copy in copies:
        copy.start()

    def lay_tile(tile):
        slot = lax.rem(tile, 2)
        turned = jnp.transpose(links_ref[tile])
        for k in range(offsets):
            cols[slot, k] = jnp.broadcast_to(turned[:, k : k + 1], (TILE, LANES))
        start = pl.multiple_of(tile * TILE, TILE)
        feat_t[slot] = jnp.transpose(feat_ref[pl.ds(start, TILE), :])

    lane = lax.broadcasted_iota(jnp.int32, (1, LANES), 1)

    def gather(step, base_of):
        tile = step // groups
        group = lax.rem(step, groups)
        slot = lax.rem(tile, 2)
        bases = [base_of(j) for j in range(SEGS)]
        names = []
        for half in range(SEGS * SEG // LANES):
            per = LANES // SEG
            name = lane
            for j in range(per):
                off = bases[half * per + j] * SEG - j * SEG
                name = jnp.where(lane // SEG == j, lane + off, name)
            names.append(name)
        source = jnp.concatenate(
            [
                table[pl.ds(pl.multiple_of(jnp.maximum(b, 0) * SEG, SEG), SEG), :]
                for b in bases
            ],
            axis=0,
        )
        found = []
        for z in range(3):
            col = cols[slot, 3 * group + z]
            hot = [jnp.where(col == name, 1.0, 0.0).astype(BF) for name in names]
            found.append(
                jnp.dot(
                    jnp.concatenate(hot, axis=1), source, preferred_element_type=F32
                ).astype(BF)
            )
        return found

    def first_gather(step):
        found = gather(step, lambda j: seg_ref[step, j])
        buf = lax.rem(step, 2)
        for z in range(3):
            picked[buf, z] = found[z]

    def more_gather(step):
        count = pass_ref[step]

        @pl.when(count > 1)
        def _():
            @pl.loop(1, count)
            def _(p):
                @pl.when(p >= LISTED)
                def _():
                    copy = pltpu.make_async_copy(all_segs.at[step, p], spill, spill_sem)
                    copy.start()
                    copy.wait()

                @pl.when(p < LISTED)
                def _():
                    for j in range(SEGS):
                        spill[j] = seg_ref[step, p * SEGS + j]

                found = gather(step, lambda j: spill[j])
                buf = lax.rem(step, 2)
                for z in range(3):
                    picked[buf, z] += found[z]

    def products(step):
        tile = step // groups
        group = lax.rem(step, groups)
        slot = lax.rem(tile, 2)
        buf = lax.rem(step, 2)
        total = acc[...]
        for z in range(3):
            k = offsets - 1 - (3 * group + z)
            got = picked[buf, z]
            total = total + lax.dot_general(
                got, w_ref[k], (((1,), (1,)), ((), ())), preferred_element_type=F32
            )
            wg_ref[k] += jnp.dot(feat_t[slot], got, preferred_element_type=F32)
        acc[...] = total

    wg_ref[...] = jnp.zeros_like(wg_ref)
    acc[...] = jnp.zeros_like(acc)
    lay_tile(0)
    for copy in copies:
        copy.wait()
    first_gather(0)
    more_gather(0)
    steps = tiles * groups

    @pl.loop(0, steps)
    def _(step):
        tile = step // groups
        group = lax.rem(step, groups)
        following = jnp.minimum(step + 1, steps - 1)

        @pl.when((group == groups - 1) & (tile < tiles - 1))
        def _():
            lay_tile(tile + 1)

        first_gather(following)
        products(step)

        @pl.when(group == groups - 1)
        def _():
            start = pl.multiple_of(tile * TILE, TILE)
            left = rows - (tiles - 1) * TILE

            @pl.when(tile < tiles - 1)
            def _():
                in_ref[pl.ds(start, TILE), :] = acc[...].astype(BF)

            @pl.when(tile == tiles - 1)
            def _():
                in_ref[pl.ds((tiles - 1) * TILE, left), :] = acc[:left, :].astype(BF)

            acc[...] = jnp.zeros_like(acc)

        @pl.when(step + 1 < steps)
        def _():
            more_gather(following)


def convolve(plan, dz, mid, low, high, feat, weight):
    laid, listed, passes = plan
    rows, chans = dz.shape
    width = mid.shape[1]
    offsets = weight.shape[0]
    tiles = laid.shape[0]
    hbm = pl.BlockSpec(memory_space=pl.ANY)
    vmem = pl.BlockSpec(memory_space=pltpu.VMEM)
    smem = pl.BlockSpec(memory_space=pltpu.SMEM)
    listed_first = listed[:, :LISTED].reshape(listed.shape[0], LISTED * SEGS)
    feat = jnp.pad(feat, ((0, tiles * TILE - rows), (0, 0)))
    return pl.pallas_call(
        functools.partial(conv_kernel, rows, width),
        out_shape=(
            jax.ShapeDtypeStruct((rows, chans), BF),
            jax.ShapeDtypeStruct((offsets, chans, chans), F32),
        ),
        in_specs=[smem, smem, hbm, vmem, hbm, hbm, hbm, hbm, vmem, vmem],
        out_specs=(vmem, vmem),
        scratch_shapes=[
            pltpu.VMEM((rows + 9 * width, chans), BF),
            pltpu.VMEM((2, offsets, TILE, LANES), jnp.int32),
            pltpu.VMEM((2, chans, TILE), BF),
            pltpu.VMEM((TILE, chans), F32),
            pltpu.VMEM((2, 3, TILE, chans), BF),
            pltpu.SMEM((SEGS,), jnp.int32),
            pltpu.SemaphoreType.DMA((10,)),
            pltpu.SemaphoreType.DMA,
        ],
        compiler_params=pltpu.CompilerParams(vmem_limit_bytes=50 << 20),
        cost_estimate=pl.CostEstimate(
            flops=6 * offsets * rows * chans * chans,
            bytes_accessed=30 << 20,
            transcendentals=0,
        ),
    )(listed_first, passes, listed, laid, dz, mid, low, high, feat, weight)


def body(features, pre_norm, out_grad, weight, gamma, beta, neighbors, boundary, counts):
    feat = features[0, 0]
    rows, chans = feat.shape
    border = boundary[0, 0]
    links = neighbors[0, 0]
    width = border.shape[0]
    tiles = -(-rows // TILE)
    plan = plan_segments(links, rows, width, tiles)
    live = (lax.iota(jnp.int32, rows) < counts[0, 0])[:, None]
    zval = pre_norm[0, 0].astype(F32)
    zlive = jnp.where(live, zval, F32(0.0))
    own = jnp.stack(
        [
            jnp.sum(zlive, axis=0),
            jnp.sum(zlive * zval, axis=0),
            jnp.broadcast_to(counts[0, 0].astype(F32), (chans,)),
        ]
    )
    sums = everyone_sum(own)
    count = sums[2]
    mean = sums[0] / count
    var = sums[1] / count - mean * mean
    rstd = lax.rsqrt(var + 1e-05)
    zhat = (zval - mean) * rstd
    act = gamma * zhat + beta
    sig = jax.nn.sigmoid(act)
    grad_act = jnp.where(
        live, out_grad[0, 0].astype(F32) * sig * (1.0 + act * (1.0 - sig)), F32(0.0)
    )
    grads = everyone_sum(
        jnp.stack([jnp.sum(grad_act, axis=0), jnp.sum(grad_act * zhat, axis=0)])
    )
    beta_grad, gamma_grad = grads[0], grads[1]
    dz = jnp.where(
        live,
        gamma * rstd * (grad_act - beta_grad / count - zhat * gamma_grad / count),
        F32(0.0),
    ).astype(BF)
    edge = jnp.where(
        (border < rows)[:, None], jnp.take(dz, border, axis=0, mode="clip"), BF(0.0)
    )
    below, above = shift(edge, "gx")
    mid = jnp.stack([below, edge, above])
    low, high = shift(mid, "gy")
    in_grad, wgrad = convolve(plan, dz, mid, low, high, feat, weight)
    weight_grad = scatter_sum(wgrad.reshape(-1, chans))
    return (in_grad[None, None], weight_grad.reshape(-1, chans), gamma_grad, beta_grad)


def solution(mesh):
    placed = (
        P("gx", "gy", None, None),
        P("gx", "gy", None, None),
        P("gx", "gy", None, None),
        P(),
        P(),
        P(),
        P("gx", "gy", None, None),
        P("gx", "gy", None),
        P("gx", "gy"),
    )
    return jax.shard_map(
        body,
        mesh=mesh,
        in_specs=placed,
        out_specs=(P("gx", "gy", None, None), P(("gx", "gy"), None), P(), P()),
        check_vma=False,
    )
```

time: 701 us -> 198 us (0.28)
  local copies, waits for them, and re-layouts: 332 us -> 14.2 us
  matrix products: 92.1 us -> 0 us
  waiting for transfers between devices: 136 us -> 48.5 us
  blocking collectives: 82.9 us -> 0 us
  Pallas kernels: 0 us -> 75.4 us
  starting transfers between devices: 11.6 us -> 38.3 us
  between operations: 14.8 us -> 1.84 us
  other arithmetic: 26.1 us -> 18.6 us
    gather x28 -> x1, local copies, waits for them, and re-layouts: 257 us -> 2.81 us  [body(): jnp.take(dz, border, axis=0, mode='clip')]
    reduce_scatter x1 -> x0, waiting for transfers between devices: 122 us -> none  [body(): lax.psum_scatter(local_wgrad, ('gx', 'gy'), scatter_dimension=0, tiled=True)]
    dot_general x54 -> x0, matrix products: 92.1 us -> none  [the longest x27 46.3 us: offset_step(): lax.dot_general(picked, w_k, (((1,), (1,)), ((), ())), preferred_element_...]
    psum x2 -> x0, blocking collectives: 82.9 us -> none  [the longest x1 42.7 us: body(): lax.psum((jnp.sum(zlive, axis=0), jnp.sum(zlive * zval, axis=0), counts[0...]
    pallas_call x0 -> x1, Pallas kernels: none -> 75.4 us  [convolve(): pl.pallas_call(functools.partial(conv_kernel, rows, width), out_shape=(ja...]
    dynamic_update_slice x54 -> x0, local copies, waits for them, and re-layouts: 42.3 us -> none  [body(): lax.scan(offset_step, jnp.zeros((rows, chans), jnp.float32), (links[::-1]...]
    ppermute x4 -> x13, waiting for transfers between devices: 13.4 us -> 37.7 us  [the longest x9 23.7 us: halve(): got = lax.ppermute(give, axis, [(i, i ^ 1 << bit) for i in range(count)])]
    dynamic_slice x27 -> x0, local copies, waits for them, and re-layouts: 22.9 us -> none  [body(): lax.scan(offset_step, jnp.zeros((rows, chans), jnp.float32), (links[::-1]...]
  transfers between devices with their start and end apart: 5 -> 15, of which waited for: 3 -> 10; matrix products, arithmetic and copies ran while one was open for 2% -> 8% of each run, Pallas kernels for 0% -> 0%
where the time goes in v1:
time: 198 us; the launch traced here: 197 us
  Pallas kernels  75.4 us (38%)
  waiting for transfers between devices  48.5 us (24%)
  starting transfers between devices  38.3 us (19%)
  other arithmetic  18.6 us (9%)
  local copies, waits for them, and re-layouts  14.2 us (7%)
    pallas_call x1, Pallas kernels, convolve(): pl.pallas_call(functools.partial(conv_kernel, rows, width), out_shape=(ja...  75.4 us
    ppermute x9, waiting for transfers between devices, halve(): got = lax.ppermute(give, axis, [(i, i ^ 1 << bit) for i in range(count)])  23.7 us
    ppermute x9, starting transfers between devices, halve(): got = lax.ppermute(give, axis, [(i, i ^ 1 << bit) for i in range(count)])  21 us
    ppermute x2, waiting for transfers between devices, shift(): lax.ppermute(block, axis, forward)  14.1 us
    all_to_all x2, waiting for transfers between devices, everyone_sum(): return jnp.sum(lax.all_to_all(spread, AXES, 0, 0, tiled=True), axis=0)  10.8 us
    all_to_all x2, starting transfers between devices, everyone_sum(): return jnp.sum(lax.all_to_all(spread, AXES, 0, 0, tiled=True), axis=0)  9.9 us
    add x9, other arithmetic, halve(): return keep + got.astype(F32)  4.81 us
    ppermute x2, starting transfers between devices, shift(): lax.ppermute(block, axis, forward)  4.81 us
  transfers between devices with their start and end apart: 15, of which 10 were waited for; matrix products, arithmetic and copies ran while one was open for 8% of the time, Pallas kernels for 0%

profile of v1, /device:TPU:0, one launch (start us, length us, event | category | flops | bytes accessed | tf_op | source)
XLA Modules:
  0.0 196.8 jit_solution(15250095629021691312)
XLA Ops:
  4.0 7.3 %all-to-all-start = ((f32[32,3,256]{2,1,0:T(4,128)}), f32[32,3,256]{2,1,0:T(4,128)S(1)}, u32[]{:S(2)}, u32[]{:S(2)}) async-start(f32[32,3,256]{2,1,0:T(4,128)} %broadcast_in_dim.115), calls=%async_computation | async-start | bytes 262144 | tf_op jit(solution)/shard_map/all_to_all | solution.py:24
  12.5 3.3 %select_reduce_fusion.2 = (s32[9,11]{1,0:T(8,128)S(1)}, s32[9,11]{1,0:T(8,128)S(1)}, s32[9,11]{1,0:T(8,128)S(1)}, s32[9,11]{1,0:T(8,128)}, s32[9,11]{1,0:T(8,128...) fusion(s32[9,3,11,192]{3,2,1,0:T(8,128)S(1)} %reshape.1231), kind=kLoop, calls=%fused_computation.46 | loop fusion | flops 3989700 | bytes 236016 | tf_op jit(solution)/shard_map/reduce_max | solution.py:86
  16.0 3.5 %all-to-all-done = f32[32,3,256]{2,1,0:T(4,128)S(1)} async-done(((f32[32,3,256]{2,1,0:T(4,128)}), f32[32,3,256]{2,1,0:T(4,128)S(1)}, u32[]{:S(2)}, u32[]{:S(2)}) %all-to-all-start) | async-done | bytes 98336 | tf_op jit(solution)/shard_map/all_to_all | solution.py:24
  19.6 2.4 %fusion.122 = (f32[256]{0:T(256)S(1)}, f32[256]{0:T(256)S(1)}, f32[2048,256]{1,0:T(8,128)}) fusion(f32[256]{0:T(256)S(1)} %bitcast.491, f32[256]{0:T(256)S(1)} %bitcast.493, bf16[1,1,2048,256]{3,2,1,0:T(8,128)(2,1)S(1)} %copy-done, f32[256]{0:T(256)S(1)} %copy-done.9, f32[256]{0:T(256)S(1)} %copy-done.7, bf16[1,1,2048,256]{3,2,1,0:T(8,128)(2,1)S(1)} %copy-done.1, ...), kind=kLoop, calls=%fused_computation.351 | loop fusion | flops 9436672 | bytes 4202496 | tf_op jit(solution)/shard_map/reduce_sum | solution.py:339
  22.7 2.6 %all-to-all-start.1 = ((f32[32,2,256]{2,1,0:T(2,128)}), f32[32,2,256]{2,1,0:T(2,128)S(1)}, u32[]{:S(2)}, u32[]{:S(2)}) async-start(f32[32,2,256]{2,1,0:T(2,128)} %broadcast_in_dim.116), calls=%async_computation.1 | async-start | bytes 131072 | tf_op jit(solution)/shard_map/all_to_all | solution.py:24
  25.3 7.4 %all-to-all-done.1 = f32[32,2,256]{2,1,0:T(2,128)S(1)} async-done(((f32[32,2,256]{2,1,0:T(2,128)}), f32[32,2,256]{2,1,0:T(2,128)S(1)}, u32[]{:S(2)}, u32[]{:S(2)}) %all-to-all-start.1) | async-done | bytes 65568 | tf_op jit(solution)/shard_map/all_to_all | solution.py:24
  35.3 2.8 %gather_fusion = bf16[704,256]{1,0:T(8,128)(2,1)S(1)} fusion(bf16[2048,256]{1,0:T(8,128)(2,1)S(1)} %fusion.21.dz_ref, s32[1024]{0:T(1024)S(1)} %pad_clamp_fusion), kind=kCustom, calls=%fused_computation | custom fusion | bytes 723712 | tf_op jit(solution)/shard_map/jit(_take)/gather | solution.py:348
  38.3 2.5 %collective-permute-start = (bf16[704,256]{1,0:T(8,128)(2,1)S(1)}, bf16[704,256]{1,0:T(8,128)(2,1)S(1)}, u32[]{:S(2)}, u32[]{:S(2)}) collective-permute-start(bf16[704,256]{1,0:T(8,128)(2,1)S(1)} %broadcast_select_fusion), channel_id=1, source_target_pairs={{0,4},{4,8},{8,12},{12,16},{16,20},{20,24},{24,28},{1,5},{5,9},{9,... | collective-permute-start | bytes 1081352 | tf_op jit(solution)/shard_map/ppermute | solution.py:31
  42.3 14.1 %collective-permute-done = bf16[704,256]{1,0:T(8,128)(2,1)S(1)} collective-permute-done((bf16[704,256]{1,0:T(8,128)(2,1)S(1)}, bf16[704,256]{1,0:T(8,128)(2,1)S(1)}, u32[]{:S(2)}, u32[]{:S(2)}) %collective-permute-start) | collective-permute-done | bytes 360480 | tf_op jit(solution)/shard_map/ppermute | solution.py:31
  56.5 2.3 %collective-permute-start.2 = (bf16[3,704,256]{2,1,0:T(8,128)(2,1)S(1)}, bf16[3,704,256]{2,1,0:T(8,128)(2,1)}, u32[]{:S(2)}, u32[]{:S(2)}) collective-permute-start(bf16[3,704,256]{2,1,0:T(8,128)(2,1)S(1)} %pad_maximum_fusion.mid_ref), channel_id=1, source_target_pairs={{0,1},{1,2},{2,3},{4,5},{5,6},{6,7},{8,9},{9,10},{10,11},{12,13},{... | collective-permute-start | bytes 3244040 | tf_op jit(solution)/shard_map/ppermute | solution.py:31
  62.0 2.1 %copy.42.all_segs = s32[99,33,16]{2,1,0:T(8,128)} copy(s32[99,33,16]{0,2,1:T(8,128)S(1)} %bitcast.481) | data formatting | bytes 418176 | tf_op jit(solution)/shard_map/sub | solution.py:97
  64.5 2.3 %pad.14.feat_ref = bf16[2112,256]{1,0:T(8,128)(2,1)} pad(bf16[2048,256]{1,0:T(8,128)(2,1)} %bitcast.483, bf16[]{:T(256)} %constant.271.clone.1), padding=0_64x0_0 | pad | bytes 2129922 | tf_op jit(solution)/shard_map/jit(_pad)/pad | solution.py:281
  66.8 75.4 %shard_map.120 = (bf16[2048,256]{1,0:T(8,128)(2,1)}, f32[27,256,256]{2,1,0:T(8,128)}) custom-call(s32[99,48]{1,0:T(8,128)S(1)} %copy.41.seg_ref, s32[99]{0:T(128)S(1)} %and_select_fusion.pass_ref, s32[99,33,16]{2,1,0:T(8,128)} %copy.42.all_segs, s32[11,32,192]{2,1,0:T(8,128)S(1)} %pad.13.links_ref, bf16[2048,256]{1,0:T(8,128)(2,1)S(1)} %fusion.21.dz_ref, ...), custom_call_target="tpu_custom_call" | custom-call | flops 21743271936 | bytes 31457280 | tf_op jit(solution)/shard_map/pallas_call | solution.py:282
  142.2 2.2 %fusion.22 = bf16[2,2,2,2,216,256]{5,4,0,1,3,2:T(8,128)(2,1)S(1)} fusion(f32[2,2,2,2,2,216,256]{6,5,4,3,2,1,0:T(8,128)} %bitcast.478, s32[]{:T(128)S(6)} %select_n.543), kind=kLoop, calls=%fused_computation.32 | loop fusion | bytes 3538948 | tf_op jit(solution)/shard_map/convert_element_type | solution.py:37
  144.4 9.6 %collective-permute-start.4 = (bf16[2,2,2,2,216,256]{5,4,0,1,3,2:T(8,128)(2,1)S(1)}, bf16[2,2,2,2,216,256]{5,4,0,1,3,2:T(8,128)(2,1)S(1)}, u32[]{:S(2)}, u32[]{:S(2)}) collective-permute-start(bf16[2,2,2,2,216,256]{5,4,0,1,3,2:T(8,128)(2,1)S(1)} %fusion.22), channel_id=1, source_target_pairs={{0,1},{1,0},{2,3},{3,2},{4,5},{5,4},{6,7},{7,6},{8,9},{9,8},{10,11... | collective-permute-start | bytes 5308424 | tf_op jit(solution)/shard_map/ppermute | solution.py:38
  154.0 3.3 %collective-permute-done.4 = bf16[2,2,2,2,216,256]{5,4,0,1,3,2:T(8,128)(2,1)S(1)} collective-permute-done((bf16[2,2,2,2,216,256]{5,4,0,1,3,2:T(8,128)(2,1)S(1)}, bf16[2,2,2,2,216,256]{5,4,0,1,3,2:T(8,128)(2,1)S(1)}, u32[]{:S(2)}, u32[]{:S(2)}) %collective-permute-start.4) | collective-permute-done | bytes 1769504 | tf_op jit(solution)/shard_map/ppermute | solution.py:38
  157.3 2.5 %bitcast_add_fusion = f32[2,2,2,2,216,256]{5,4,0,1,3,2:T(8,128)S(1)} fusion(bf16[2,2,2,2,216,256]{5,4,0,1,3,2:T(8,128)(2,1)S(1)} %collective-permute-done.4, f32[2,2,2,2,2,216,256]{6,5,4,3,2,1,0:T(8,128)} %bitcast.479, s32[]{:T(128)S(6)} %select_n.542), kind=kLoop, calls=%fused_computation.2 | loop fusion | flops 1769472 | bytes 8847364 | tf_op jit(solution)/shard_map/add | solution.py:40
  164.0 9.7 %collective-permute-done.5 = bf16[2,2,2,216,128]{4,3,0,1,2:T(8,128)(2,1)} collective-permute-done((bf16[2,2,2,216,128]{4,3,0,1,2:T(8,128)(2,1)}, bf16[2,2,2,216,128]{4,3,0,1,2:T(8,128)(2,1)}, u32[]{:S(2)}, u32[]{:S(2)}) %collective-permute-start.5) | collective-permute-done | bytes 442400 | tf_op jit(solution)/shard_map/ppermute | solution.py:38
  174.8 2.3 %collective-permute-start.6 = (bf16[2,2,216,128]{3,2,0,1:T(8,128)(2,1)S(1)}, bf16[2,2,216,128]{3,2,0,1:T(8,128)(2,1)S(1)}, u32[]{:S(2)}, u32[]{:S(2)}) collective-permute-start(bf16[2,2,216,128]{3,2,0,1:T(8,128)(2,1)S(1)} %fusion.25), channel_id=1, source_target_pairs={{0,4},{4,0},{8,12},{12,8},{16,20},{20,16},{24,28},{28,24},{1,5},{5... | collective-permute-start | bytes 663560 | tf_op jit(solution)/shard_map/ppermute | solution.py:38
  178.6 3.6 %collective-permute-done.6 = bf16[2,2,216,128]{3,2,0,1:T(8,128)(2,1)S(1)} collective-permute-done((bf16[2,2,216,128]{3,2,0,1:T(8,128)(2,1)S(1)}, bf16[2,2,216,128]{3,2,0,1:T(8,128)(2,1)S(1)}, u32[]{:S(2)}, u32[]{:S(2)}) %collective-permute-start.6) | collective-permute-done | bytes 221216 | tf_op jit(solution)/shard_map/ppermute | solution.py:38
  182.3 3.2 %collective-permute-start.7 = (bf16[2,216,128]{2,1,0:T(8,128)(2,1)S(1)}, bf16[2,216,128]{2,1,0:T(8,128)(2,1)S(1)}, u32[]{:S(2)}, u32[]{:S(2)}) collective-permute-start(bf16[2,216,128]{2,1,0:T(8,128)(2,1)S(1)} %fusion.27), channel_id=1, source_target_pairs={{0,8},{4,12},{8,0},{12,4},{16,24},{20,28},{24,16},{28,20},{1,9},{5... | collective-permute-start | bytes 331784 | tf_op jit(solution)/shard_map/ppermute | solution.py:38
  186.7 2.3 %collective-permute-done.7 = bf16[2,216,128]{2,1,0:T(8,128)(2,1)S(1)} collective-permute-done((bf16[2,216,128]{2,1,0:T(8,128)(2,1)S(1)}, bf16[2,216,128]{2,1,0:T(8,128)(2,1)S(1)}, u32[]{:S(2)}, u32[]{:S(2)}) %collective-permute-start.7) | collective-permute-done | bytes 110624 | tf_op jit(solution)/shard_map/ppermute | solution.py:38
  192.1 2.0 %collective-permute-done.8 = bf16[216,128]{1,0:T(8,128)(2,1)S(1)} collective-permute-done((bf16[216,128]{1,0:T(8,128)(2,1)S(1)}, bf16[216,128]{1,0:T(8,128)(2,1)S(1)}, u32[]{:S(2)}, u32[]{:S(2)}) %collective-permute-start.8) | collective-permute-done | bytes 55328 | tf_op jit(solution)/shard_map/ppermute | solution.py:38
  194.1 2.0 %collective-permute-done.12 = bf16[216,128]{1,0:T(8,128)(2,1)S(1)} collective-permute-done((bf16[216,128]{1,0:T(8,128)(2,1)S(1)}, bf16[216,128]{1,0:T(8,128)(2,1)S(1)}, u32[]{:S(2)}, u32[]{:S(2)}) %collective-permute-start.12) | collective-permute-done | bytes 55328 | tf_op jit(solution)/shard_map/ppermute | solution.py:38
  (99 shorter events, 24.6 us)
Async XLA Ops:
  0.6 15.2 %copy-start.6 = (s32[1,1,704]{2,1,0:T(1,128)S(1)}, s32[1,1,704]{2,1,0:T(1,128)}, u32[]{:S(2)}) copy-start(s32[1,1,704]{2,1,0:T(1,128)} %param.16) | copy-start | bytes 8452
  1.3 18.3 %copy-start = (bf16[1,1,2048,256]{3,2,1,0:T(8,128)(2,1)S(1)}, bf16[1,1,2048,256]{3,2,1,0:T(8,128)(2,1)}, u32[]{:S(2)}) copy-start(bf16[1,1,2048,256]{3,2,1,0:T(8,128)(2,1)} %param.10) | copy-start | bytes 3145732
  1.3 18.2 %copy-start.1 = (bf16[1,1,2048,256]{3,2,1,0:T(8,128)(2,1)S(1)}, bf16[1,1,2048,256]{3,2,1,0:T(8,128)(2,1)}, u32[]{:S(2)}) copy-start(bf16[1,1,2048,256]{3,2,1,0:T(8,128)(2,1)} %param.11) | copy-start | bytes 3145732
  1.3 18.2 %copy-start.7 = (f32[256]{0:T(256)S(1)}, f32[256]{0:T(256)}, u32[]{:S(2)}) copy-start(f32[256]{0:T(256)} %param.13) | copy-start | bytes 3076
  1.3 18.2 %copy-start.9 = (f32[256]{0:T(256)S(1)}, f32[256]{0:T(256)}, u32[]{:S(2)}) copy-start(f32[256]{0:T(256)} %param.14) | copy-start | bytes 3076
  4.0 15.5 %all-to-all-start = ((f32[32,3,256]{2,1,0:T(4,128)}), f32[32,3,256]{2,1,0:T(4,128)S(1)}, u32[]{:S(2)}, u32[]{:S(2)}) async-start(f32[32,3,256]{2,1,0:T(4,128)} %broadcast_in_dim.115), calls=%async_computation | async-start | bytes 262144 | tf_op jit(solution)/shard_map/all_to_all | solution.py:24
  22.7 10.0 %all-to-all-start.1 = ((f32[32,2,256]{2,1,0:T(2,128)}), f32[32,2,256]{2,1,0:T(2,128)S(1)}, u32[]{:S(2)}, u32[]{:S(2)}) async-start(f32[32,2,256]{2,1,0:T(2,128)} %broadcast_in_dim.116), calls=%async_computation.1 | async-start | bytes 131072 | tf_op jit(solution)/shard_map/all_to_all | solution.py:24
  38.1 22.0 %copy-start.4 = (s32[9,11]{1,0:T(8,128)S(1)}, s32[9,11]{1,0:T(8,128)}, u32[]{:S(2)}) copy-start(s32[9,11]{1,0:T(8,128)} %get-tuple-element.15) | copy-start | bytes 1192
  38.1 22.0 %copy-start.5 = (s32[9,11]{1,0:T(8,128)S(1)}, s32[9,11]{1,0:T(8,128)}, u32[]{:S(2)}) copy-start(s32[9,11]{1,0:T(8,128)} %get-tuple-element.16) | copy-start | bytes 1192
  38.3 18.1 %collective-permute-start = (bf16[704,256]{1,0:T(8,128)(2,1)S(1)}, bf16[704,256]{1,0:T(8,128)(2,1)S(1)}, u32[]{:S(2)}, u32[]{:S(2)}) collective-permute-start(bf16[704,256]{1,0:T(8,128)(2,1)S(1)} %broadcast_select_fusion), channel_id=1, source_target_pairs={{0,4},{4,8},{8,12},{12,16},{16,20},{20,24},{24,28},{1,5},{5,9},{9,... | collective-permute-start | bytes 1081352 | tf_op jit(solution)/shard_map/ppermute | solution.py:31
  40.8 15.6 %collective-permute-start.1 = (bf16[704,256]{1,0:T(8,128)(2,1)S(1)}, bf16[704,256]{1,0:T(8,128)(2,1)S(1)}, u32[]{:S(2)}, u32[]{:S(2)}) collective-permute-start(bf16[704,256]{1,0:T(8,128)(2,1)S(1)} %broadcast_select_fusion), channel_id=1, source_target_pairs={{4,0},{8,4},{12,8},{16,12},{20,16},{24,20},{28,24},{5,1},{9,5},{13... | collective-permute-start | bytes 1081352 | tf_op jit(solution)/shard_map/ppermute | solution.py:31
  42.2 14.2 %copy-start.2 = (s32[9,11,10]{1,0,2:T(8,128)}, s32[9,11,10]{1,0,2:T(8,128)S(1)}, u32[]{:S(2)}) copy-start(s32[9,11,10]{1,0,2:T(8,128)S(1)} %get-tuple-element.42) | copy-start | bytes 11884
  56.4 3.7 %copy-start.3 = (s32[9,11,10]{1,0,2:T(8,128)S(1)}, s32[9,11,10]{1,0,2:T(8,128)}, u32[]{:S(2)}) copy-start(s32[9,11,10]{1,0,2:T(8,128)} %copy-done.2) | copy-start | bytes 11884
  56.5 10.3 %collective-permute-start.2 = (bf16[3,704,256]{2,1,0:T(8,128)(2,1)S(1)}, bf16[3,704,256]{2,1,0:T(8,128)(2,1)}, u32[]{:S(2)}, u32[]{:S(2)}) collective-permute-start(bf16[3,704,256]{2,1,0:T(8,128)(2,1)S(1)} %pad_maximum_fusion.mid_ref), channel_id=1, source_target_pairs={{0,1},{1,2},{2,3},{4,5},{5,6},{6,7},{8,9},{9,10},{10,11},{12,13},{... | collective-permute-start | bytes 3244040 | tf_op jit(solution)/shard_map/ppermute | solution.py:31
  58.8 8.0 %collective-permute-start.3 = (bf16[3,704,256]{2,1,0:T(8,128)(2,1)S(1)}, bf16[3,704,256]{2,1,0:T(8,128)(2,1)}, u32[]{:S(2)}, u32[]{:S(2)}) collective-permute-start(bf16[3,704,256]{2,1,0:T(8,128)(2,1)S(1)} %pad_maximum_fusion.mid_ref), channel_id=1, source_target_pairs={{1,0},{2,1},{3,2},{5,4},{6,5},{7,6},{9,8},{10,9},{11,10},{13,12},{... | collective-permute-start | bytes 3244040 | tf_op jit(solution)/shard_map/ppermute | solution.py:31
  144.4 12.9 %collective-permute-start.4 = (bf16[2,2,2,2,216,256]{5,4,0,1,3,2:T(8,128)(2,1)S(1)}, bf16[2,2,2,2,216,256]{5,4,0,1,3,2:T(8,128)(2,1)S(1)}, u32[]{:S(2)}, u32[]{:S(2)}) collective-permute-start(bf16[2,2,2,2,216,256]{5,4,0,1,3,2:T(8,128)(2,1)S(1)} %fusion.22), channel_id=1, source_target_pairs={{0,1},{1,0},{2,3},{3,2},{4,5},{5,4},{6,7},{7,6},{8,9},{9,8},{10,11... | collective-permute-start | bytes 5308424 | tf_op jit(solution)/shard_map/ppermute | solution.py:38
  160.9 12.8 %collective-permute-start.5 = (bf16[2,2,2,216,128]{4,3,0,1,2:T(8,128)(2,1)}, bf16[2,2,2,216,128]{4,3,0,1,2:T(8,128)(2,1)}, u32[]{:S(2)}, u32[]{:S(2)}) collective-permute-start(bf16[2,2,2,216,128]{4,3,0,1,2:T(8,128)(2,1)} %fusion.23), channel_id=1, source_target_pairs={{0,2},{1,3},{2,0},{3,1},{4,6},{5,7},{6,4},{7,5},{8,10},{9,11},{10,... | collective-permute-start | bytes 1327112 | tf_op jit(solution)/shard_map/ppermute | solution.py:38
  162.6 14.5 %collective-permute-start.9 = (bf16[2,2,2,216,128]{4,3,0,1,2:T(8,128)(2,1)}, bf16[2,2,2,216,128]{4,3,0,1,2:T(8,128)(2,1)}, u32[]{:S(2)}, u32[]{:S(2)}) collective-permute-start(bf16[2,2,2,216,128]{4,3,0,1,2:T(8,128)(2,1)} %fusion.24), channel_id=1, source_target_pairs={{0,4},{4,0},{8,12},{12,8},{16,20},{20,16},{24,28},{28,24},{1,5},{5... | collective-permute-start | bytes 1327112 | tf_op jit(solution)/shard_map/ppermute | solution.py:38
  174.8 7.4 %collective-permute-start.6 = (bf16[2,2,216,128]{3,2,0,1:T(8,128)(2,1)S(1)}, bf16[2,2,216,128]{3,2,0,1:T(8,128)(2,1)S(1)}, u32[]{:S(2)}, u32[]{:S(2)}) collective-permute-start(bf16[2,2,216,128]{3,2,0,1:T(8,128)(2,1)S(1)} %fusion.25), channel_id=1, source_target_pairs={{0,4},{4,0},{8,12},{12,8},{16,20},{20,16},{24,28},{28,24},{1,5},{5... | collective-permute-start | bytes 663560 | tf_op jit(solution)/shard_map/ppermute | solution.py:38
  178.2 7.2 %collective-permute-start.10 = (bf16[2,2,216,128]{3,2,0,1:T(8,128)(2,1)S(1)}, bf16[2,2,216,128]{3,2,0,1:T(8,128)(2,1)S(1)}, u32[]{:S(2)}, u32[]{:S(2)}) collective-permute-start(bf16[2,2,216,128]{3,2,0,1:T(8,128)(2,1)S(1)} %fusion.26), channel_id=1, source_target_pairs={{0,2},{1,3},{2,0},{3,1},{4,6},{5,7},{6,4},{7,5},{8,10},{9,11},{10,... | collective-permute-start | bytes 663560 | tf_op jit(solution)/shard_map/ppermute | solution.py:38
  182.3 6.7 %collective-permute-start.7 = (bf16[2,216,128]{2,1,0:T(8,128)(2,1)S(1)}, bf16[2,216,128]{2,1,0:T(8,128)(2,1)S(1)}, u32[]{:S(2)}, u32[]{:S(2)}) collective-permute-start(bf16[2,216,128]{2,1,0:T(8,128)(2,1)S(1)} %fusion.27), channel_id=1, source_target_pairs={{0,8},{4,12},{8,0},{12,4},{16,24},{20,28},{24,16},{28,20},{1,9},{5... | collective-permute-start | bytes 331784 | tf_op jit(solution)/shard_map/ppermute | solution.py:38
  185.5 5.4 %collective-permute-start.11 = (bf16[2,216,128]{2,1,0:T(8,128)(2,1)S(1)}, bf16[2,216,128]{2,1,0:T(8,128)(2,1)S(1)}, u32[]{:S(2)}, u32[]{:S(2)}) collective-permute-start(bf16[2,216,128]{2,1,0:T(8,128)(2,1)S(1)} %fusion.28), channel_id=1, source_target_pairs={{0,8},{4,12},{8,0},{12,4},{16,24},{20,28},{24,16},{28,20},{1,9},{5... | collective-permute-start | bytes 331784 | tf_op jit(solution)/shard_map/ppermute | solution.py:38
  189.0 5.1 %collective-permute-start.8 = (bf16[216,128]{1,0:T(8,128)(2,1)S(1)}, bf16[216,128]{1,0:T(8,128)(2,1)S(1)}, u32[]{:S(2)}, u32[]{:S(2)}) collective-permute-start(bf16[216,128]{1,0:T(8,128)(2,1)S(1)} %fusion.29), channel_id=1, source_target_pairs={{0,16},{4,20},{8,24},{12,28},{16,0},{20,4},{24,8},{28,12},{1,17},{... | collective-permute-start | bytes 165896 | tf_op jit(solution)/shard_map/ppermute | solution.py:38
  191.0 5.1 %collective-permute-start.12 = (bf16[216,128]{1,0:T(8,128)(2,1)S(1)}, bf16[216,128]{1,0:T(8,128)(2,1)S(1)}, u32[]{:S(2)}, u32[]{:S(2)}) collective-permute-start(bf16[216,128]{1,0:T(8,128)(2,1)S(1)} %fusion.30), channel_id=1, source_target_pairs={{0,16},{4,20},{8,24},{12,28},{16,0},{20,4},{24,8},{28,12},{1,17},{... | collective-permute-start | bytes 165896 | tf_op jit(solution)/shard_map/ppermute | solution.py:38
  (1 other events, 2.0 us)

commit v2 on v0

v2 whole, which is shorter than its diff:
```python
import functools

import jax
import jax.numpy as jnp
from jax import lax
from jax.experimental import pallas as pl
from jax.experimental.pallas import tpu as pltpu
from jax.sharding import PartitionSpec as P


TILE = 192
SEG = 16
LANES = 128
SEGS = 16
LISTED = 2
NOWHERE = -(1 << 20)
BF = jnp.bfloat16
F32 = jnp.float32
AXES = ("gx", "gy")


def everyone_sum(vec):
    count = lax.axis_size(AXES)
    spread = jnp.broadcast_to(vec[None], (count,) + vec.shape)
    return jnp.sum(lax.all_to_all(spread, AXES, 0, 0, tiled=True), axis=0)


def shift(block, axis):
    count = lax.axis_size(axis)
    forward = [(i, i + 1) for i in range(count - 1)]
    backward = [(target, source) for source, target in forward]
    return lax.ppermute(block, axis, forward), lax.ppermute(block, axis, backward)


def halve(arr, dim, axis, bit):
    count = lax.axis_size(axis)
    mine = (lax.axis_index(axis) >> bit) & 1
    give = lax.dynamic_index_in_dim(arr, 1 - mine, dim, keepdims=False).astype(BF)
    got = lax.ppermute(give, axis, [(i, i ^ (1 << bit)) for i in range(count)])
    keep = lax.dynamic_index_in_dim(arr, mine, dim, keepdims=False)
    return keep + got.astype(F32)


def scatter_sum(full):
    size_x, size_y = lax.axis_size("gx"), lax.axis_size("gy")
    rows, chans = full.shape
    bits_x, bits_y = size_x.bit_length() - 1, size_y.bit_length() - 1
    part = rows // (size_x * size_y)
    if (1 << bits_x) != size_x or (1 << bits_y) != size_y or bits_x < 1 or bits_y < 2:
        return lax.psum_scatter(full, AXES, scatter_dimension=0, tiled=True)
    arr = full.reshape((2,) * (bits_x + bits_y) + (part, chans))
    order = [("gx", b) for b in reversed(range(bits_x))] + [
        ("gy", b) for b in reversed(range(bits_y))
    ]

    def step(arr, order, which):
        dim = order.index(which)
        return halve(arr, dim, *which), order[:dim] + order[dim + 1 :]

    arr, order = step(arr, order, ("gy", 0))
    pair = [("gy", 1), ("gx", 0)]
    rest = [("gy", b) for b in range(2, bits_y)] + [("gx", b) for b in range(1, bits_x)]
    half = chans // 2
    colours = [(arr[..., :half], order), (arr[..., half:], order)]
    plans = [pair + rest, pair[::-1] + rest]
    for at in range(len(plans[0])):
        colours = [step(a, o, plan[at]) for (a, o), plan in zip(colours, plans)]
    return jnp.concatenate([a for a, _ in colours], axis=-1)


def plan_segments(links, rows, width, tiles):
    offsets = links.shape[0]
    total = rows + 9 * width
    groups = offsets // 3
    clean = jnp.where(links < total, links, NOWHERE)
    clean = jnp.pad(clean, ((0, 0), (0, tiles * TILE - rows)), constant_values=NOWHERE)
    clean = clean.reshape(offsets, tiles, TILE)
    laid = jnp.pad(
        clean.transpose(1, 0, 2), ((0, 0), (0, -offsets % 8), (0, 0)), constant_values=NOWHERE
    )
    view = clean.reshape(groups, 3, tiles, TILE)
    lows, highs = [], []
    for stretch in range(10):
        first = 0 if stretch == 0 else rows + (stretch - 1) * width
        last = rows + stretch * width
        inside = (view >= first) & (view < last)
        lows.append(jnp.min(jnp.where(inside, view, total), axis=(1, 3)))
        highs.append(jnp.max(jnp.where(inside, view, -1), axis=(1, 3)))
    low, high = jnp.stack(lows) // SEG, jnp.stack(highs)
    sizes = jnp.where(high >= 0, high // SEG - low + 1, 0)
    order = lax.iota(jnp.int32, 10)
    upto = (order[None, :] <= order[:, None])[:, :, None, None]
    ends = jnp.sum(jnp.where(upto, sizes[None], 0), axis=1)
    starts = ends - sizes
    slot = lax.iota(jnp.int32, LISTED * SEGS).reshape(-1, 1, 1, 1)
    hit = (slot >= starts[None]) & (slot < ends[None])
    listed = jnp.sum(jnp.where(hit, low[None] + slot - starts[None] + 1, 0), axis=1) - 1
    return laid, listed, low, ends


def gather_kernel(rows, width, listed_ref, first_ref, end_ref, links_ref, *refs):
    (own_ref, *lines), (out_ref, table, spill, sems) = refs[:4], refs[4:]
    tile = pl.program_id(0)
    offsets = out_ref.shape[0]
    groups = offsets // 3

    @pl.when(tile == 0)
    def _():
        copies = [pltpu.make_async_copy(own_ref, table.at[pl.ds(0, rows)], sems.at[9])]
        for da in range(3):
            for db, line in enumerate((lines[1], lines[0], lines[2])):
                at = 3 * da + db
                place = table.at[pl.ds(rows + at * width, width)]
                copies.append(pltpu.make_async_copy(line.at[da], place, sems.at[at]))
        for copy in copies:
            copy.start()
        for copy in copies:
            copy.wait()

    lane = lax.broadcasted_iota(jnp.int32, (1, LANES), 1)
    turned = jnp.transpose(links_ref[0])

    def source_of(bases):
        names = []
        per = LANES // SEG
        for half in range(SEGS // per):
            name = lane
            for j in range(per):
                off = bases[half * per + j] * SEG - j * SEG
                name = jnp.where(lane // SEG == j, lane + off, name)
            names.append(name)
        source = jnp.concatenate(
            [
                table[pl.ds(pl.multiple_of(jnp.maximum(b, 0) * SEG, SEG), SEG), :]
                for b in bases
            ],
            axis=0,
        )
        return names, source

    def pick(col, names, source):
        hot = [jnp.where(col == name, 1.0, 0.0).astype(BF) for name in names]
        return jnp.dot(
            jnp.concatenate(hot, axis=1), source, preferred_element_type=F32
        ).astype(BF)

    most = jnp.int32(0)
    for group in range(groups):
        names, source = source_of([listed_ref[j, group, tile] for j in range(SEGS)])
        for z in range(3):
            k = 3 * group + z
            col = jnp.broadcast_to(turned[:, k : k + 1], (TILE, LANES))
            out_ref[offsets - 1 - k] = pick(col, names, source)
        most = jnp.maximum(most, end_ref[9, group, tile])

    @pl.when(most > SEGS)
    def _():
        @pl.loop(0, groups)
        def _(group):
            count = (end_ref[9, group, tile] + SEGS - 1) // SEGS

            @pl.loop(1, count)
            def _(p):
                @pl.when(p < LISTED)
                def _():
                    for j in range(SEGS):
                        spill[j] = listed_ref[p * SEGS + j, group, tile]

                @pl.when(p >= LISTED)
                def _():
                    @pl.loop(0, SEGS)
                    def _(j):
                        slot = p * SEGS + j
                        base = jnp.int32(-1)
                        start = jnp.int32(0)
                        for block in range(10):
                            end = end_ref[block, group, tile]
                            here = (slot >= start) & (slot < end)
                            first = first_ref[block, group, tile]
                            base = jnp.where(here, first + slot - start, base)
                            start = end
                        spill[j] = base

                names, source = source_of([spill[j] for j in range(SEGS)])
                which = lax.broadcasted_iota(jnp.int32, turned.shape, 1)
                for z in range(3):
                    k = 3 * group + z
                    col = jnp.sum(
                        jnp.where(which == k, turned, 0), axis=1, keepdims=True
                    )
                    more = pick(jnp.broadcast_to(col, (TILE, LANES)), names, source)
                    out_ref[offsets - 1 - k] += more


def gather_all(plan, offsets, pieces):
    laid, listed, low, ends = plan
    rows, chans = pieces[0].shape
    width = pieces[1].shape[1]
    tiles = laid.shape[0]
    smem = pl.BlockSpec(memory_space=pltpu.SMEM)
    return pl.pallas_call(
        functools.partial(gather_kernel, rows, width),
        grid=(tiles,),
        out_shape=jax.ShapeDtypeStruct((offsets, rows, chans), BF),
        in_specs=[smem, smem, smem]
        + [pl.BlockSpec((1,) + laid.shape[1:], lambda i: (i, 0, 0))]
        + [pl.BlockSpec(memory_space=pl.ANY)] * 4,
        out_specs=pl.BlockSpec((offsets, TILE, chans), lambda i: (0, i, 0)),
        scratch_shapes=[
            pltpu.VMEM((rows + 9 * width, chans), BF),
            pltpu.SMEM((SEGS,), jnp.int32),
            pltpu.SemaphoreType.DMA((10,)),
        ],
        compiler_params=pltpu.CompilerParams(vmem_limit_bytes=56 << 20),
        cost_estimate=pl.CostEstimate(
            flops=2 * offsets * rows * chans * SEGS * SEG,
            bytes_accessed=2 * offsets * rows * chans,
            transcendentals=0,
        ),
    )(listed, low, ends, laid, *pieces)


def outer_kernel(turned_ref, got_ref, out_ref):
    chans = turned_ref.shape[0]
    for k in range(got_ref.shape[0]):
        out_ref[k * chans : (k + 1) * chans] = jnp.dot(
            turned_ref[...], got_ref[k], preferred_element_type=F32
        )


def outer_products(turned, got):
    chans, rows = turned.shape
    offsets = got.shape[0]
    return pl.pallas_call(
        outer_kernel,
        grid=(offsets // 3,),
        out_shape=jax.ShapeDtypeStruct((offsets * chans, chans), F32),
        in_specs=[
            pl.BlockSpec((chans, rows), lambda k: (0, 0)),
            pl.BlockSpec((3, rows, chans), lambda k: (k, 0, 0)),
        ],
        out_specs=pl.BlockSpec((3 * chans, chans), lambda k: (k, 0)),
        compiler_params=pltpu.CompilerParams(vmem_limit_bytes=56 << 20),
        cost_estimate=pl.CostEstimate(
            flops=2 * offsets * rows * chans * chans,
            bytes_accessed=2 * offsets * rows * chans,
            transcendentals=0,
        ),
    )(turned, got)


def back_kernel(got_ref, w_ref, out_ref):
    offsets = w_ref.shape[0]
    total = lax.dot_general(
        jnp.concatenate([got_ref[k] for k in range(offsets)], axis=1),
        jnp.concatenate([w_ref[k] for k in range(offsets)], axis=1),
        (((1,), (1,)), ((), ())),
        preferred_element_type=F32,
    )
    out_ref[...] = total.astype(BF)


def back_products(got, weight, first, last):
    offsets, chans, _ = weight.shape
    count = last - first
    block = 256 if count % 256 == 0 else count
    return pl.pallas_call(
        back_kernel,
        grid=(count // block,),
        out_shape=jax.ShapeDtypeStruct((count, chans), BF),
        in_specs=[
            pl.BlockSpec((offsets, block, chans), lambda i: (0, i + first // block, 0)),
            pl.BlockSpec(weight.shape, lambda i: (0, 0, 0)),
        ],
        out_specs=pl.BlockSpec((block, chans), lambda i: (i, 0)),
        compiler_params=pltpu.CompilerParams(vmem_limit_bytes=56 << 20),
        cost_estimate=pl.CostEstimate(
            flops=2 * offsets * count * chans * chans,
            bytes_accessed=2 * offsets * count * chans,
            transcendentals=0,
        ),
    )(got, weight)


def table_pieces(own, border):
    edge = jnp.take(own, border, axis=0, mode="clip")
    below, above = shift(edge, "gx")
    line = jnp.stack([below, edge, above])
    low, high = shift(line, "gy")
    return own, line, low, high


def step(features, pre_norm, out_grad, weight, gamma, beta, neighbors, boundary, counts):
    feat = features[0, 0]
    rows, chans = feat.shape
    border = boundary[0, 0]
    links = neighbors[0, 0]
    offsets = links.shape[0]
    width = border.shape[0]
    tiles = -(-rows // TILE)
    plan = plan_segments(links, rows, width, tiles)
    turned = feat.T
    live = (lax.iota(jnp.int32, rows) < counts[0, 0])[:, None]
    zval = pre_norm[0, 0].astype(F32)
    zlive = jnp.where(live, zval, F32(0.0))
    own = jnp.stack(
        [
            jnp.sum(zlive, axis=0),
            jnp.sum(zlive * zval, axis=0),
            jnp.broadcast_to(counts[0, 0].astype(F32), (chans,)),
        ]
    )
    sums = everyone_sum(own)
    count = sums[2]
    mean = sums[0] / count
    var = sums[1] / count - mean * mean
    rstd = lax.rsqrt(var + 1e-05)
    zhat = (zval - mean) * rstd
    act = gamma * zhat + beta
    sig = jax.nn.sigmoid(act)
    grad_act = jnp.where(
        live, out_grad[0, 0].astype(F32) * sig * (1.0 + act * (1.0 - sig)), F32(0.0)
    )
    pair = jnp.stack([jnp.sum(grad_act, axis=0), jnp.sum(grad_act * zhat, axis=0)])
    grads = everyone_sum(pair)
    beta_grad, gamma_grad = grads[0], grads[1]
    dz = jnp.where(
        live,
        gamma * rstd * (grad_act - beta_grad / count - zhat * gamma_grad / count),
        F32(0.0),
    ).astype(BF)
    pieces = table_pieces(dz, border)
    near = gather_all(plan, offsets, pieces)
    wgrad = outer_products(turned, near)
    weight_grad = scatter_sum(wgrad)
    cut = rows // 8 * 5
    in_grad = [back_products(near, weight, 0, cut)]
    in_grad.append(back_products(near, weight, cut, rows))
    in_grad = jnp.concatenate(in_grad)
    return (in_grad[None, None], weight_grad.reshape(-1, chans), gamma_grad, beta_grad)


def solution(mesh):
    placed = (
        P("gx", "gy", None, None),
        P("gx", "gy", None, None),
        P("gx", "gy", None, None),
        P(),
        P(),
        P(),
        P("gx", "gy", None, None),
        P("gx", "gy", None),
        P("gx", "gy"),
    )
    return jax.shard_map(
        step,
        mesh=mesh,
        in_specs=placed,
        out_specs=(P("gx", "gy", None, None), P(("gx", "gy"), None), P(), P()),
        check_vma=False,
    )
```

time: 701 us -> 181 us (0.26)
  local copies, waits for them, and re-layouts: 332 us -> 14 us
  waiting for transfers between devices: 136 us -> 42.4 us
  matrix products: 92.1 us -> 0 us
  blocking collectives: 82.9 us -> 0 us
  Pallas kernels: 0 us -> 64.4 us
  starting transfers between devices: 11.6 us -> 39.6 us
  between operations: 14.8 us -> 1.9 us
  other arithmetic: 26.1 us -> 18.4 us
    gather x28 -> x1, local copies, waits for them, and re-layouts: 257 us -> 2.81 us  [table_pieces(): edge = jnp.take(own, border, axis=0, mode='clip')]
    reduce_scatter x1 -> x0, waiting for transfers between devices: 122 us -> none  [body(): lax.psum_scatter(local_wgrad, ('gx', 'gy'), scatter_dimension=0, tiled=True)]
    dot_general x54 -> x0, matrix products: 92.1 us -> none  [the longest x27 46.3 us: offset_step(): lax.dot_general(picked, w_k, (((1,), (1,)), ((), ())), preferred_element_...]
    psum x2 -> x0, blocking collectives: 82.9 us -> none  [the longest x1 42.7 us: body(): lax.psum((jnp.sum(zlive, axis=0), jnp.sum(zlive * zval, axis=0), counts[0...]
    pallas_call x0 -> x4, Pallas kernels: none -> 64.4 us  [the longest x1 27.1 us: gather_all(): pl.pallas_call(functools.partial(gather_kernel, rows, width), grid=(tiles...]
    dynamic_update_slice x54 -> x0, local copies, waits for them, and re-layouts: 42.3 us -> none  [body(): lax.scan(offset_step, jnp.zeros((rows, chans), jnp.float32), (links[::-1]...]
    dynamic_slice x27 -> x0, local copies, waits for them, and re-layouts: 22.9 us -> none  [body(): lax.scan(offset_step, jnp.zeros((rows, chans), jnp.float32), (links[::-1]...]
    ppermute x4 -> x13, waiting for transfers between devices: 13.4 us -> 32.5 us  [the longest x9 19.4 us: halve(): got = lax.ppermute(give, axis, [(i, i ^ 1 << bit) for i in range(count)])]
  transfers between devices with their start and end apart: 5 -> 15, of which waited for: 3 -> 10; matrix products, arithmetic and copies ran while one was open for 2% -> 7% of each run, Pallas kernels for 0% -> 11%
where the time goes in v2:
time: 181 us
  Pallas kernels  64.4 us (36%)
  waiting for transfers between devices  42.4 us (23%)
  starting transfers between devices  39.6 us (22%)
  other arithmetic  18.4 us (10%)
  local copies, waits for them, and re-layouts  14 us (8%)
  between operations  1.9 us (1%)
    pallas_call x1, Pallas kernels, gather_all(): pl.pallas_call(functools.partial(gather_kernel, rows, width), grid=(tiles...  27.1 us
    pallas_call x2, Pallas kernels, back_products(): pl.pallas_call(back_kernel, grid=(count // block,), out_shape=jax.ShapeDt...  19.4 us
    ppermute x9, waiting for transfers between devices, halve(): got = lax.ppermute(give, axis, [(i, i ^ 1 << bit) for i in range(count)])  19.4 us
    ppermute x9, starting transfers between devices, halve(): got = lax.ppermute(give, axis, [(i, i ^ 1 << bit) for i in range(count)])  19.3 us
    pallas_call x1, Pallas kernels, outer_products(): pl.pallas_call(outer_kernel, grid=(offsets // 3,), out_shape=jax.ShapeDty...  17.9 us
    all_to_all x2, starting transfers between devices, everyone_sum(): return jnp.sum(lax.all_to_all(spread, AXES, 0, 0, tiled=True), axis=0)  9.9 us
    all_to_all x2, waiting for transfers between devices, everyone_sum(): return jnp.sum(lax.all_to_all(spread, AXES, 0, 0, tiled=True), axis=0)  9.84 us
    ppermute x2, starting transfers between devices, shift(): lax.ppermute(block, axis, forward)  7.55 us
  transfers between devices with their start and end apart: 15, of which 10 were waited for; matrix products, arithmetic and copies ran while one was open for 7% of the time, Pallas kernels for 11%

profile of v2, /device:TPU:0, one launch (start us, length us, event | category | flops | bytes accessed | tf_op | source)
XLA Modules:
  0.0 180.7 jit_solution(11957745595412365310)
XLA Ops:
  3.9 7.3 %all-to-all-start = ((f32[32,3,256]{2,1,0:T(4,128)}), f32[32,3,256]{2,1,0:T(4,128)S(1)}, u32[]{:S(2)}, u32[]{:S(2)}) async-start(f32[32,3,256]{2,1,0:T(4,128)} %broadcast_in_dim.115), calls=%async_computation | async-start | bytes 262144 | tf_op jit(solution)/shard_map/all_to_all | solution.py:25
  12.5 3.4 %select_reduce_fusion.12 = (s32[9,11]{1,0:T(8,128)S(1)}, s32[9,11]{1,0:T(8,128)S(1)}, s32[9,11]{1,0:T(8,128)S(1)}, s32[9,11]{1,0:T(8,128)S(1)}, s32[9,11]{1,0:T(...) fusion(s32[9,3,11,192]{3,2,1,0:T(8,128)S(1)} %reshape_reshape.3), kind=kLoop, calls=%fused_computation.57 | loop fusion | flops 3989700 | bytes 236016 | tf_op jit(solution)/shard_map/reduce_max | solution.py:88
  16.1 3.4 %all-to-all-done = f32[32,3,256]{2,1,0:T(4,128)S(1)} async-done(((f32[32,3,256]{2,1,0:T(4,128)}), f32[32,3,256]{2,1,0:T(4,128)S(1)}, u32[]{:S(2)}, u32[]{:S(2)}) %all-to-all-start) | async-done | bytes 98336 | tf_op jit(solution)/shard_map/all_to_all | solution.py:25
  19.6 2.4 %fusion.38 = (f32[256]{0:T(256)S(1)}, f32[256]{0:T(256)S(1)}, f32[2048,256]{1,0:T(8,128)}) fusion(f32[256]{0:T(256)S(1)} %bitcast.129, f32[256]{0:T(256)S(1)} %bitcast.131, bf16[1,1,2048,256]{3,2,1,0:T(8,128)(2,1)S(1)} %copy-done.1, f32[256]{0:T(256)S(1)} %copy-done.12, f32[256]{0:T(256)S(1)} %copy-done.9, bf16[1,1,2048,256]{3,2,1,0:T(8,128)(2,1)S(1)} %copy-done.7, ...), kind=kLoop, calls=%fused_computation.142 | loop fusion | flops 9436672 | bytes 4202496 | tf_op jit(solution)/shard_map/reduce_sum | solution.py:324
  22.7 2.6 %all-to-all-start.1 = ((f32[32,2,256]{2,1,0:T(2,128)}), f32[32,2,256]{2,1,0:T(2,128)S(1)}, u32[]{:S(2)}, u32[]{:S(2)}) async-start(f32[32,2,256]{2,1,0:T(2,128)} %broadcast_in_dim.116), calls=%async_computation.1 | async-start | bytes 131072 | tf_op jit(solution)/shard_map/all_to_all | solution.py:25
  26.2 6.4 %all-to-all-done.1 = f32[32,2,256]{2,1,0:T(2,128)S(1)} async-done(((f32[32,2,256]{2,1,0:T(2,128)}), f32[32,2,256]{2,1,0:T(2,128)S(1)}, u32[]{:S(2)}, u32[]{:S(2)}) %all-to-all-start.1) | async-done | bytes 65568 | tf_op jit(solution)/shard_map/all_to_all | solution.py:25
  35.3 2.8 %gather_fusion = bf16[704,256]{1,0:T(8,128)(2,1)S(1)} fusion(bf16[2048,256]{1,0:T(8,128)(2,1)S(1)} %fusion.20.refs_0_, s32[1024]{0:T(1024)S(1)} %pad_clamp_fusion), kind=kCustom, calls=%fused_computation | custom fusion | bytes 723712 | tf_op jit(solution)/shard_map/jit(_take)/gather | solution.py:286
  39.6 4.6 %collective-permute-start = (bf16[704,256]{1,0:T(8,128)(2,1)S(1)}, bf16[704,256]{1,0:T(8,128)(2,1)S(1)}, u32[]{:S(2)}, u32[]{:S(2)}) collective-permute-start(bf16[704,256]{1,0:T(8,128)(2,1)S(1)} %gather_fusion), channel_id=1, source_target_pairs={{0,4},{4,8},{8,12},{12,16},{16,20},{20,24},{24,28},{1,5},{5,9},{9,... | collective-permute-start | bytes 1081352 | tf_op jit(solution)/shard_map/ppermute | solution.py:32
  44.2 6.4 %collective-permute-done.1 = bf16[704,256]{1,0:T(8,128)(2,1)S(1)} collective-permute-done((bf16[704,256]{1,0:T(8,128)(2,1)S(1)}, bf16[704,256]{1,0:T(8,128)(2,1)S(1)}, u32[]{:S(2)}, u32[]{:S(2)}) %collective-permute-start.1) | collective-permute-done | bytes 360480 | tf_op jit(solution)/shard_map/ppermute | solution.py:32
  50.6 6.7 %collective-permute-done = bf16[704,256]{1,0:T(8,128)(2,1)S(1)} collective-permute-done((bf16[704,256]{1,0:T(8,128)(2,1)S(1)}, bf16[704,256]{1,0:T(8,128)(2,1)S(1)}, u32[]{:S(2)}, u32[]{:S(2)}) %collective-permute-start) | collective-permute-done | bytes 360480 | tf_op jit(solution)/shard_map/ppermute | solution.py:32
  57.4 3.0 %collective-permute-start.2 = (bf16[3,704,256]{2,1,0:T(8,128)(2,1)S(1)}, bf16[3,704,256]{2,1,0:T(8,128)(2,1)}, u32[]{:S(2)}, u32[]{:S(2)}) collective-permute-start(bf16[3,704,256]{2,1,0:T(8,128)(2,1)S(1)} %pad_maximum_fusion.refs_1_), channel_id=1, source_target_pairs={{0,1},{1,2},{2,3},{4,5},{5,6},{6,7},{8,9},{9,10},{10,11},{12,13},{... | collective-permute-start | bytes 3244040 | tf_op jit(solution)/shard_map/ppermute | solution.py:32
  64.3 2.3 %copy.40 = bf16[1,1,2048,256]{2,3,1,0:T(8,128)(2,1)} copy(bf16[1,1,2048,256]{3,2,1,0:T(8,128)(2,1)} %param.9) | data formatting | bytes 2097152 | tf_op args[0]
  68.3 27.1 %shard_map.120.got_ref = bf16[27,2048,256]{2,1,0:T(8,128)(2,1)} custom-call(s32[32,9,11]{2,1,0:T(8,128)} %broadcast_add_fusion.listed_ref, s32[10,9,11]{2,1,0:T(8,128)} %copy-done.8, s32[10,9,11]{2,1,0:T(8,128)} %copy-done.5, s32[11,32,192]{2,1,0:T(8,128)} %pad.9.links_ref, bf16[2048,256]{1,0:T(8,128)(2,1)} %copy-done, bf16[3,704,256]{2,1,0:T(8,128)(2,1)} %copy-done.2, ...), custom_call_target="tpu_custom_call" | custom-call | flops 7247757312 | bytes 28311552 | tf_op jit(solution)/shard_map/pallas_call | solution.py:201
  95.4 17.9 %shard_map.123 = f32[6912,256]{1,0:T(8,128)} custom-call(bf16[256,2048]{1,0:T(8,128)(2,1)} %bitcast.122, bf16[27,2048,256]{2,1,0:T(8,128)(2,1)} %shard_map.120.got_ref), custom_call_target="tpu_custom_call" | custom-call | flops 7247757312 | bytes 28311552 | tf_op jit(solution)/shard_map/pallas_call | solution.py:234
  113.3 3.5 %fusion.21 = bf16[2,2,2,2,216,256]{5,4,0,1,3,2:T(8,128)(2,1)} fusion(f32[2,2,2,2,2,216,256]{6,5,4,3,2,1,0:T(8,128)} %bitcast.118, s32[]{:T(128)S(6)} %select_n.183), kind=kLoop, calls=%fused_computation.28 | loop fusion | bytes 3538948 | tf_op jit(solution)/shard_map/convert_element_type | solution.py:38
  116.8 8.0 %collective-permute-start.4 = (bf16[2,2,2,2,216,256]{5,4,0,1,3,2:T(8,128)(2,1)}, bf16[2,2,2,2,216,256]{5,4,0,1,3,2:T(8,128)(2,1)}, u32[]{:S(2)}, u32[]{:S(2)}) collective-permute-start(bf16[2,2,2,2,216,256]{5,4,0,1,3,2:T(8,128)(2,1)} %fusion.21), channel_id=1, source_target_pairs={{0,1},{1,0},{2,3},{3,2},{4,5},{5,4},{6,7},{7,6},{8,9},{9,8},{10,11... | collective-permute-start | bytes 5308424 | tf_op jit(solution)/shard_map/ppermute | solution.py:39
  124.9 11.4 %shard_map.121 = bf16[1280,256]{1,0:T(8,128)(2,1)} custom-call(bf16[27,2048,256]{2,1,0:T(8,128)(2,1)} %shard_map.120.got_ref, bf16[27,256,256]{2,1,0:T(8,128)(2,1)} %w_ref.3), custom_call_target="tpu_custom_call" | custom-call | flops 4529848320 | bytes 17694720 | tf_op jit(solution)/shard_map/pallas_call | solution.py:267
  138.7 2.6 %collective-permute-start.9 = (bf16[2,2,2,216,128]{4,3,0,1,2:T(8,128)(2,1)S(1)}, bf16[2,2,2,216,128]{4,3,0,1,2:T(8,128)(2,1)S(1)}, u32[]{:S(2)}, u32[]{:S(2)}) collective-permute-start(bf16[2,2,2,216,128]{4,3,0,1,2:T(8,128)(2,1)S(1)} %fusion.24), channel_id=1, source_target_pairs={{0,4},{4,0},{8,12},{12,8},{16,20},{20,16},{24,28},{28,24},{1,5},{5... | collective-permute-start | bytes 1327112 | tf_op jit(solution)/shard_map/ppermute | solution.py:39
  141.2 8.0 %shard_map.122 = bf16[768,256]{1,0:T(8,128)(2,1)} custom-call(bf16[27,2048,256]{2,1,0:T(8,128)(2,1)} %shard_map.120.got_ref, bf16[27,256,256]{2,1,0:T(8,128)(2,1)} %w_ref.3), custom_call_target="tpu_custom_call" | custom-call | flops 2717908992 | bytes 10616832 | tf_op jit(solution)/shard_map/pallas_call | solution.py:267
  153.7 8.8 %collective-permute-done.5 = bf16[2,2,2,216,128]{4,3,0,1,2:T(8,128)(2,1)S(1)} collective-permute-done((bf16[2,2,2,216,128]{4,3,0,1,2:T(8,128)(2,1)S(1)}, bf16[2,2,2,216,128]{4,3,0,1,2:T(8,128)(2,1)S(1)}, u32[]{:S(2)}, u32[]{:S(2)}) %collective-permute-start.5) | collective-permute-done | bytes 442400 | tf_op jit(solution)/shard_map/ppermute | solution.py:39
  162.7 3.2 %collective-permute-done.10 = bf16[2,2,216,128]{3,2,0,1:T(8,128)(2,1)S(1)} collective-permute-done((bf16[2,2,216,128]{3,2,0,1:T(8,128)(2,1)S(1)}, bf16[2,2,216,128]{3,2,0,1:T(8,128)(2,1)S(1)}, u32[]{:S(2)}, u32[]{:S(2)}) %collective-permute-start.10) | collective-permute-done | bytes 221216 | tf_op jit(solution)/shard_map/ppermute | solution.py:39
  166.0 2.9 %collective-permute-start.11 = (bf16[2,216,128]{2,1,0:T(8,128)(2,1)S(1)}, bf16[2,216,128]{2,1,0:T(8,128)(2,1)S(1)}, u32[]{:S(2)}, u32[]{:S(2)}) collective-permute-start(bf16[2,216,128]{2,1,0:T(8,128)(2,1)S(1)} %fusion.28), channel_id=1, source_target_pairs={{0,8},{4,12},{8,0},{12,4},{16,24},{20,28},{24,16},{28,20},{1,9},{5... | collective-permute-start | bytes 331784 | tf_op jit(solution)/shard_map/ppermute | solution.py:39
  169.0 2.6 %collective-permute-start.7 = (bf16[2,216,128]{2,1,0:T(8,128)(2,1)S(1)}, bf16[2,216,128]{2,1,0:T(8,128)(2,1)S(1)}, u32[]{:S(2)}, u32[]{:S(2)}) collective-permute-start(bf16[2,216,128]{2,1,0:T(8,128)(2,1)S(1)} %fusion.27), channel_id=1, source_target_pairs={{0,8},{4,12},{8,0},{12,4},{16,24},{20,28},{24,16},{28,20},{1,9},{5... | collective-permute-start | bytes 331784 | tf_op jit(solution)/shard_map/ppermute | solution.py:39
  175.7 2.1 %collective-permute-done.12 = bf16[216,128]{1,0:T(8,128)(2,1)S(1)} collective-permute-done((bf16[216,128]{1,0:T(8,128)(2,1)S(1)}, bf16[216,128]{1,0:T(8,128)(2,1)S(1)}, u32[]{:S(2)}, u32[]{:S(2)}) %collective-permute-start.12) | collective-permute-done | bytes 55328 | tf_op jit(solution)/shard_map/ppermute | solution.py:39
  (115 shorter events, 29.4 us)
Async XLA Ops:
  1.3 18.3 %copy-start.1 = (bf16[1,1,2048,256]{3,2,1,0:T(8,128)(2,1)S(1)}, bf16[1,1,2048,256]{3,2,1,0:T(8,128)(2,1)}, u32[]{:S(2)}) copy-start(bf16[1,1,2048,256]{3,2,1,0:T(8,128)(2,1)} %param.10) | copy-start | bytes 3145732
  1.3 18.2 %copy-start.7 = (bf16[1,1,2048,256]{3,2,1,0:T(8,128)(2,1)S(1)}, bf16[1,1,2048,256]{3,2,1,0:T(8,128)(2,1)}, u32[]{:S(2)}) copy-start(bf16[1,1,2048,256]{3,2,1,0:T(8,128)(2,1)} %param.11) | copy-start | bytes 3145732
  1.3 18.2 %copy-start.9 = (f32[256]{0:T(256)S(1)}, f32[256]{0:T(256)}, u32[]{:S(2)}) copy-start(f32[256]{0:T(256)} %param.13) | copy-start | bytes 3076
  1.3 18.2 %copy-start.12 = (f32[256]{0:T(256)S(1)}, f32[256]{0:T(256)}, u32[]{:S(2)}) copy-start(f32[256]{0:T(256)} %param.14) | copy-start | bytes 3076
  3.9 15.5 %all-to-all-start = ((f32[32,3,256]{2,1,0:T(4,128)}), f32[32,3,256]{2,1,0:T(4,128)S(1)}, u32[]{:S(2)}, u32[]{:S(2)}) async-start(f32[32,3,256]{2,1,0:T(4,128)} %broadcast_in_dim.115), calls=%async_computation | async-start | bytes 262144 | tf_op jit(solution)/shard_map/all_to_all | solution.py:25
  22.7 10.0 %all-to-all-start.1 = ((f32[32,2,256]{2,1,0:T(2,128)}), f32[32,2,256]{2,1,0:T(2,128)S(1)}, u32[]{:S(2)}, u32[]{:S(2)}) async-start(f32[32,2,256]{2,1,0:T(2,128)} %broadcast_in_dim.116), calls=%async_computation.1 | async-start | bytes 131072 | tf_op jit(solution)/shard_map/all_to_all | solution.py:25
  35.3 22.1 %copy-start = (bf16[2048,256]{1,0:T(8,128)(2,1)}, bf16[2048,256]{1,0:T(8,128)(2,1)S(1)}, u32[]{:S(2)}) copy-start(bf16[2048,256]{1,0:T(8,128)(2,1)S(1)} %fusion.20.refs_0_) | copy-start | bytes 3145732
  38.1 25.2 %copy-start.4 = (s32[27,11,192]{2,1,0:T(8,128)S(1)}, s32[27,11,192]{2,1,0:T(8,128)}, u32[]{:S(2)}) copy-start(s32[27,11,192]{2,1,0:T(8,128)} %reshape.1248) | copy-start | bytes 684292
  38.1 12.5 %collective-permute-start.1 = (bf16[704,256]{1,0:T(8,128)(2,1)S(1)}, bf16[704,256]{1,0:T(8,128)(2,1)S(1)}, u32[]{:S(2)}, u32[]{:S(2)}) collective-permute-start(bf16[704,256]{1,0:T(8,128)(2,1)S(1)} %gather_fusion), channel_id=1, source_target_pairs={{4,0},{8,4},{12,8},{16,12},{20,16},{24,20},{28,24},{5,1},{9,5},{13... | collective-permute-start | bytes 1081352 | tf_op jit(solution)/shard_map/ppermute | solution.py:32
  39.6 17.7 %collective-permute-start = (bf16[704,256]{1,0:T(8,128)(2,1)S(1)}, bf16[704,256]{1,0:T(8,128)(2,1)S(1)}, u32[]{:S(2)}, u32[]{:S(2)}) collective-permute-start(bf16[704,256]{1,0:T(8,128)(2,1)S(1)} %gather_fusion), channel_id=1, source_target_pairs={{0,4},{4,8},{8,12},{12,16},{16,20},{20,24},{24,28},{1,5},{5,9},{9,... | collective-permute-start | bytes 1081352 | tf_op jit(solution)/shard_map/ppermute | solution.py:32
  57.4 9.9 %collective-permute-start.2 = (bf16[3,704,256]{2,1,0:T(8,128)(2,1)S(1)}, bf16[3,704,256]{2,1,0:T(8,128)(2,1)}, u32[]{:S(2)}, u32[]{:S(2)}) collective-permute-start(bf16[3,704,256]{2,1,0:T(8,128)(2,1)S(1)} %pad_maximum_fusion.refs_1_), channel_id=1, source_target_pairs={{0,1},{1,2},{2,3},{4,5},{5,6},{6,7},{8,9},{9,10},{10,11},{12,13},{... | collective-permute-start | bytes 3244040 | tf_op jit(solution)/shard_map/ppermute | solution.py:32
  60.4 6.9 %collective-permute-start.3 = (bf16[3,704,256]{2,1,0:T(8,128)(2,1)S(1)}, bf16[3,704,256]{2,1,0:T(8,128)(2,1)S(1)}, u32[]{:S(2)}, u32[]{:S(2)}) collective-permute-start(bf16[3,704,256]{2,1,0:T(8,128)(2,1)S(1)} %pad_maximum_fusion.refs_1_), channel_id=1, source_target_pairs={{1,0},{2,1},{3,2},{5,4},{6,5},{7,6},{9,8},{10,9},{11,10},{13,12},{... | collective-permute-start | bytes 3244040 | tf_op jit(solution)/shard_map/ppermute | solution.py:32
  113.3 23.0 %slice-start = ((s8[7077888]{0:T(1024)(128)(4,1)}), s8[2883584]{0:T(1024)(128)(4,1)S(1)}, s32[]{:S(2)}) async-start(s8[7077888]{0:T(1024)(128)(4,1)} %bitcast.119), calls=%async_computation.2 | async-start | bytes 5767168
  116.8 19.5 %collective-permute-start.4 = (bf16[2,2,2,2,216,256]{5,4,0,1,3,2:T(8,128)(2,1)}, bf16[2,2,2,2,216,256]{5,4,0,1,3,2:T(8,128)(2,1)}, u32[]{:S(2)}, u32[]{:S(2)}) collective-permute-start(bf16[2,2,2,2,216,256]{5,4,0,1,3,2:T(8,128)(2,1)} %fusion.21), channel_id=1, source_target_pairs={{0,1},{1,0},{2,3},{3,2},{4,5},{5,4},{6,7},{7,6},{8,9},{9,8},{10,11... | collective-permute-start | bytes 5308424 | tf_op jit(solution)/shard_map/ppermute | solution.py:39
  124.9 11.4 %slice-start.1 = ((s8[7077888]{0:T(1024)(128)(4,1)}), s8[4194304]{0:T(1024)(128)(4,1)S(1)}, s32[]{:S(2)}) async-start(s8[7077888]{0:T(1024)(128)(4,1)} %bitcast.119), calls=%async_computation.3 | async-start | bytes 8388608
  138.7 12.0 %copy-start.3 = (bf16[1280,256]{1,0:T(8,128)(2,1)S(1)}, bf16[1280,256]{1,0:T(8,128)(2,1)}, u32[]{:S(2)}) copy-start(bf16[1280,256]{1,0:T(8,128)(2,1)} %shard_map.121) | copy-start | bytes 1966084
  138.7 14.0 %collective-permute-start.9 = (bf16[2,2,2,216,128]{4,3,0,1,2:T(8,128)(2,1)S(1)}, bf16[2,2,2,216,128]{4,3,0,1,2:T(8,128)(2,1)S(1)}, u32[]{:S(2)}, u32[]{:S(2)}) collective-permute-start(bf16[2,2,2,216,128]{4,3,0,1,2:T(8,128)(2,1)S(1)} %fusion.24), channel_id=1, source_target_pairs={{0,4},{4,0},{8,12},{12,8},{16,20},{20,16},{24,28},{28,24},{1,5},{5... | collective-permute-start | bytes 1327112 | tf_op jit(solution)/shard_map/ppermute | solution.py:39
  149.3 13.1 %collective-permute-start.5 = (bf16[2,2,2,216,128]{4,3,0,1,2:T(8,128)(2,1)S(1)}, bf16[2,2,2,216,128]{4,3,0,1,2:T(8,128)(2,1)S(1)}, u32[]{:S(2)}, u32[]{:S(2)}) collective-permute-start(bf16[2,2,2,216,128]{4,3,0,1,2:T(8,128)(2,1)S(1)} %fusion.23), channel_id=1, source_target_pairs={{0,2},{1,3},{2,0},{3,1},{4,6},{5,7},{6,4},{7,5},{8,10},{9,11},{10,... | collective-permute-start | bytes 1327112 | tf_op jit(solution)/shard_map/ppermute | solution.py:39
  152.8 13.1 %collective-permute-start.10 = (bf16[2,2,216,128]{3,2,0,1:T(8,128)(2,1)S(1)}, bf16[2,2,216,128]{3,2,0,1:T(8,128)(2,1)S(1)}, u32[]{:S(2)}, u32[]{:S(2)}) collective-permute-start(bf16[2,2,216,128]{3,2,0,1:T(8,128)(2,1)S(1)} %fusion.26), channel_id=1, source_target_pairs={{0,2},{1,3},{2,0},{3,1},{4,6},{5,7},{6,4},{7,5},{8,10},{9,11},{10,... | collective-permute-start | bytes 663560 | tf_op jit(solution)/shard_map/ppermute | solution.py:39
  162.6 6.3 %collective-permute-start.6 = (bf16[2,2,216,128]{3,2,0,1:T(8,128)(2,1)S(1)}, bf16[2,2,216,128]{3,2,0,1:T(8,128)(2,1)S(1)}, u32[]{:S(2)}, u32[]{:S(2)}) collective-permute-start(bf16[2,2,216,128]{3,2,0,1:T(8,128)(2,1)S(1)} %fusion.25), channel_id=1, source_target_pairs={{0,4},{4,0},{8,12},{12,8},{16,20},{20,16},{24,28},{28,24},{1,5},{5... | collective-permute-start | bytes 663560 | tf_op jit(solution)/shard_map/ppermute | solution.py:39
  166.0 6.6 %collective-permute-start.11 = (bf16[2,216,128]{2,1,0:T(8,128)(2,1)S(1)}, bf16[2,216,128]{2,1,0:T(8,128)(2,1)S(1)}, u32[]{:S(2)}, u32[]{:S(2)}) collective-permute-start(bf16[2,216,128]{2,1,0:T(8,128)(2,1)S(1)} %fusion.28), channel_id=1, source_target_pairs={{0,8},{4,12},{8,0},{12,4},{16,24},{20,28},{24,16},{28,20},{1,9},{5... | collective-permute-start | bytes 331784 | tf_op jit(solution)/shard_map/ppermute | solution.py:39
  169.0 5.9 %collective-permute-start.7 = (bf16[2,216,128]{2,1,0:T(8,128)(2,1)S(1)}, bf16[2,216,128]{2,1,0:T(8,128)(2,1)S(1)}, u32[]{:S(2)}, u32[]{:S(2)}) collective-permute-start(bf16[2,216,128]{2,1,0:T(8,128)(2,1)S(1)} %fusion.27), channel_id=1, source_target_pairs={{0,8},{4,12},{8,0},{12,4},{16,24},{20,28},{24,16},{28,20},{1,9},{5... | collective-permute-start | bytes 331784 | tf_op jit(solution)/shard_map/ppermute | solution.py:39
  172.6 5.2 %collective-permute-start.12 = (bf16[216,128]{1,0:T(8,128)(2,1)S(1)}, bf16[216,128]{1,0:T(8,128)(2,1)S(1)}, u32[]{:S(2)}, u32[]{:S(2)}) collective-permute-start(bf16[216,128]{1,0:T(8,128)(2,1)S(1)} %fusion.37), channel_id=1, source_target_pairs={{0,16},{4,20},{8,24},{12,28},{16,0},{20,4},{24,8},{28,12},{1,17},{... | collective-permute-start | bytes 165896 | tf_op jit(solution)/shard_map/ppermute | solution.py:39
  174.9 5.1 %collective-permute-start.8 = (bf16[216,128]{1,0:T(8,128)(2,1)S(1)}, bf16[216,128]{1,0:T(8,128)(2,1)S(1)}, u32[]{:S(2)}, u32[]{:S(2)}) collective-permute-start(bf16[216,128]{1,0:T(8,128)(2,1)S(1)} %fusion.36), channel_id=1, source_target_pairs={{0,16},{4,20},{8,24},{12,28},{16,0},{20,4},{24,8},{28,12},{1,17},{... | collective-permute-start | bytes 165896 | tf_op jit(solution)/shard_map/ppermute | solution.py:39
  (6 other events, 27.7 us)

commit v3 on v2

--- a/solution.py
+++ b/solution.py
@@ -8,7 +8,7 @@
 from jax.sharding import PartitionSpec as P
 
 
-TILE = 192
+TILE = 176
 SEG = 16
 LANES = 128
 SEGS = 16
@@ -19,17 +19,17 @@
 AXES = ("gx", "gy")
 
 
-def everyone_sum(vec):
+def from_everyone(vec):
     count = lax.axis_size(AXES)
     spread = jnp.broadcast_to(vec[None], (count,) + vec.shape)
-    return jnp.sum(lax.all_to_all(spread, AXES, 0, 0, tiled=True), axis=0)
-
-
-def shift(block, axis):
+    return lax.all_to_all(spread, AXES, 0, 0, tiled=True)
+
+
+def shift(up, down, axis):
     count = lax.axis_size(axis)
     forward = [(i, i + 1) for i in range(count - 1)]
     backward = [(target, source) for source, target in forward]
-    return lax.ppermute(block, axis, forward), lax.ppermute(block, axis, backward)
+    return lax.ppermute(up, axis, forward), lax.ppermute(down, axis, backward)
 
 
 def halve(arr, dim, axis, bit):
@@ -74,10 +74,8 @@
     groups = offsets // 3
     clean = jnp.where(links < total, links, NOWHERE)
     clean = jnp.pad(clean, ((0, 0), (0, tiles * TILE - rows)), constant_values=NOWHERE)
-    clean = clean.reshape(offsets, tiles, TILE)
-    laid = jnp.pad(
-        clean.transpose(1, 0, 2), ((0, 0), (0, -offsets % 8), (0, 0)), constant_values=NOWHERE
-    )
+    laid = clean.reshape(groups, 3, tiles * TILE)
+    laid = jnp.pad(laid, ((0, 0), (0, 5), (0, 0)), constant_values=NOWHERE)
     view = clean.reshape(groups, 3, tiles, TILE)
     lows, highs = [], []
     for stretch in range(10):
@@ -98,27 +96,53 @@
     return laid, listed, low, ends
 
 
-def gather_kernel(rows, width, listed_ref, first_ref, end_ref, links_ref, *refs):
-    (own_ref, *lines), (out_ref, table, spill, sems) = refs[:4], refs[4:]
-    tile = pl.program_id(0)
-    offsets = out_ref.shape[0]
-    groups = offsets // 3
-
-    @pl.when(tile == 0)
+def gather_kernel(
+    rows,
+    width,
+    listed_ref,
+    first_ref,
+    end_ref,
+    begin_ref,
+    links_ref,
+    own_ref,
+    edge_ref,
+    low_ref,
+    high_ref,
+    pair_ref,
+    low_pair_ref,
+    high_pair_ref,
+    turned_ref,
+    feat_ref,
+    got_ref,
+    wg_ref,
+    table,
+    columns,
+    spill,
+    sems,
+):
+    group = pl.program_id(0)
+    chans = table.shape[1]
+    tiles = links_ref.shape[2] // TILE
+
+    @pl.when(group == 0)
     def _():
         copies = [pltpu.make_async_copy(own_ref, table.at[pl.ds(0, rows)], sems.at[9])]
-        for da in range(3):
-            for db, line in enumerate((lines[1], lines[0], lines[2])):
-                at = 3 * da + db
-                place = table.at[pl.ds(rows + at * width, width)]
-                copies.append(pltpu.make_async_copy(line.at[da], place, sems.at[at]))
+        for db, side in enumerate((low_ref, edge_ref, high_ref)):
+            place = table.at[pl.ds(rows + (3 + db) * width, width)]
+            copies.append(pltpu.make_async_copy(side, place, sems.at[3 + db]))
+        part = pair_ref.shape[1]
+        for da in range(2):
+            for db, pair in enumerate((low_pair_ref, pair_ref, high_pair_ref)):
+                at = 6 * da + db
+                start = pl.multiple_of(rows + at * width + begin_ref[at], SEG)
+                place = table.at[pl.ds(start, part)]
+                copies.append(pltpu.make_async_copy(pair.at[da], place, sems.at[at]))
         for copy in copies:
             copy.start()
         for copy in copies:
             copy.wait()
 
     lane = lax.broadcasted_iota(jnp.int32, (1, LANES), 1)
-    turned = jnp.transpose(links_ref[0])
 
     def source_of(bases):
         names = []
@@ -139,25 +163,35 @@
         return names, source
 
     def pick(col, names, source):
-        hot = [jnp.where(col == name, 1.0, 0.0).astype(BF) for name in names]
+        wide = jnp.broadcast_to(col, (col.shape[0], LANES))
+        hot = [jnp.where(wide == name, 1.0, 0.0).astype(BF) for name in names]
         return jnp.dot(
             jnp.concatenate(hot, axis=1), source, preferred_element_type=F32
         ).astype(BF)
 
+    upright = jnp.transpose(links_ref[0])
     most = jnp.int32(0)
-    for group in range(groups):
+    for tile in range(tiles):
+        start, stop = tile * TILE, min((tile + 1) * TILE, rows)
         names, source = source_of([listed_ref[j, group, tile] for j in range(SEGS)])
         for z in range(3):
-            k = 3 * group + z
-            col = jnp.broadcast_to(turned[:, k : k + 1], (TILE, LANES))
-            out_ref[offsets - 1 - k] = pick(col, names, source)
+            got_ref[2 - z, start:stop] = pick(upright[start:stop, z : z + 1], names, source)
         most = jnp.maximum(most, end_ref[9, group, tile])
+    for z in range(3):
+        wg_ref[z * chans : (z + 1) * chans] = jnp.dot(
+            turned_ref[...], got_ref[z], preferred_element_type=F32
+        )
 
     @pl.when(most > SEGS)
     def _():
-        @pl.loop(0, groups)
-        def _(group):
+        columns[...] = upright
+
+        @pl.loop(0, tiles)
+        def _(tile):
             count = (end_ref[9, group, tile] + SEGS - 1) // SEGS
+            start = pl.multiple_of(jnp.minimum(tile * TILE, rows - TILE), SEG)
+            row = start + lax.broadcasted_iota(jnp.int32, (TILE, 1), 0)
+            fresh = row >= tile * TILE
 
             @pl.loop(1, count)
             def _(p):
@@ -172,81 +206,64 @@
                     def _(j):
                         slot = p * SEGS + j
                         base = jnp.int32(-1)
-                        start = jnp.int32(0)
+                        begin = jnp.int32(0)
                         for block in range(10):
                             end = end_ref[block, group, tile]
-                            here = (slot >= start) & (slot < end)
+                            here = (slot >= begin) & (slot < end)
                             first = first_ref[block, group, tile]
-                            base = jnp.where(here, first + slot - start, base)
-                            start = end
+                            base = jnp.where(here, first + slot - begin, base)
+                            begin = end
                         spill[j] = base
 
                 names, source = source_of([spill[j] for j in range(SEGS)])
-                which = lax.broadcasted_iota(jnp.int32, turned.shape, 1)
+                beside = feat_ref[pl.ds(start, TILE), :]
                 for z in range(3):
-                    k = 3 * group + z
-                    col = jnp.sum(
-                        jnp.where(which == k, turned, 0), axis=1, keepdims=True
+                    col = columns[pl.ds(start, TILE), z : z + 1]
+                    more = pick(jnp.where(fresh, col, NOWHERE), names, source)
+                    got_ref[2 - z, pl.ds(start, TILE)] += more
+                    wg_ref[(2 - z) * chans : (3 - z) * chans] += lax.dot_general(
+                        beside, more, (((0,), (0,)), ((), ())), preferred_element_type=F32
                     )
-                    more = pick(jnp.broadcast_to(col, (TILE, LANES)), names, source)
-                    out_ref[offsets - 1 - k] += more
-
-
-def gather_all(plan, offsets, pieces):
+
+
+def gather_outer(plan, pieces, feat, turned):
     laid, listed, low, ends = plan
-    rows, chans = pieces[0].shape
-    width = pieces[1].shape[1]
-    tiles = laid.shape[0]
+    rows, chans = feat.shape
+    begins, *pieces = pieces
+    width = pieces[1].shape[0]
+    groups = laid.shape[0]
     smem = pl.BlockSpec(memory_space=pltpu.SMEM)
     return pl.pallas_call(
         functools.partial(gather_kernel, rows, width),
-        grid=(tiles,),
-        out_shape=jax.ShapeDtypeStruct((offsets, rows, chans), BF),
-        in_specs=[smem, smem, smem]
-        + [pl.BlockSpec((1,) + laid.shape[1:], lambda i: (i, 0, 0))]
-        + [pl.BlockSpec(memory_space=pl.ANY)] * 4,
-        out_specs=pl.BlockSpec((offsets, TILE, chans), lambda i: (0, i, 0)),
+        grid=(groups,),
+        out_shape=(
+            jax.ShapeDtypeStruct((3 * groups, rows, chans), BF),
+            jax.ShapeDtypeStruct((3 * groups * chans, chans), F32),
+        ),
+        in_specs=[smem] * 4
+        + [pl.BlockSpec((1,) + laid.shape[1:], lambda g: (g, 0, 0))]
+        + [pl.BlockSpec(memory_space=pl.ANY)] * 7
+        + [
+            pl.BlockSpec((chans, rows), lambda g: (0, 0)),
+            pl.BlockSpec((rows, chans), lambda g: (0, 0)),
+        ],
+        out_specs=(
+            pl.BlockSpec((3, rows, chans), lambda g: (groups - 1 - g, 0, 0)),
+            pl.BlockSpec((3 * chans, chans), lambda g: (groups - 1 - g, 0)),
+        ),
         scratch_shapes=[
             pltpu.VMEM((rows + 9 * width, chans), BF),
+            pltpu.VMEM((laid.shape[2], laid.shape[1]), jnp.int32),
             pltpu.SMEM((SEGS,), jnp.int32),
             pltpu.SemaphoreType.DMA((10,)),
         ],
         compiler_params=pltpu.CompilerParams(vmem_limit_bytes=56 << 20),
         cost_estimate=pl.CostEstimate(
-            flops=2 * offsets * rows * chans * SEGS * SEG,
-            bytes_accessed=2 * offsets * rows * chans,
+            flops=12 * groups * rows * chans * chans,
+            bytes_accessed=6 * groups * rows * chans,
             transcendentals=0,
         ),
-    )(listed, low, ends, laid, *pieces)
-
-
-def outer_kernel(turned_ref, got_ref, out_ref):
-    chans = turned_ref.shape[0]
-    for k in range(got_ref.shape[0]):
-        out_ref[k * chans : (k + 1) * chans] = jnp.dot(
-            turned_ref[...], got_ref[k], preferred_element_type=F32
-        )
-
-
-def outer_products(turned, got):
-    chans, rows = turned.shape
-    offsets = got.shape[0]
-    return pl.pallas_call(
-        outer_kernel,
-        grid=(offsets // 3,),
-        out_shape=jax.ShapeDtypeStruct((offsets * chans, chans), F32),
-        in_specs=[
-            pl.BlockSpec((chans, rows), lambda k: (0, 0)),
-            pl.BlockSpec((3, rows, chans), lambda k: (k, 0, 0)),
-        ],
-        out_specs=pl.BlockSpec((3 * chans, chans), lambda k: (k, 0)),
-        compiler_params=pltpu.CompilerParams(vmem_limit_bytes=56 << 20),
-        cost_estimate=pl.CostEstimate(
-            flops=2 * offsets * rows * chans * chans,
-            bytes_accessed=2 * offsets * rows * chans,
-            transcendentals=0,
-        ),
-    )(turned, got)
+    )(listed, low, ends, begins, laid, *pieces, turned, feat)
 
 
 def back_kernel(got_ref, w_ref, out_ref):
@@ -282,12 +299,26 @@
     )(got, weight)
 
 
-def table_pieces(own, border):
+def window_of(used, width):
+    part = -(-(width // 2) // SEG) * SEG
+    return part, -(-jnp.maximum(used - part, 0) // SEG) * SEG
+
+
+def table_pieces(own, border, used_by):
+    rows, width = own.shape[0], border.shape[0]
+    size_x, size_y = lax.axis_size("gx"), lax.axis_size("gy")
+    at_x, at_y = lax.axis_index("gx"), lax.axis_index("gy")
+    part, start = window_of(jnp.sum((border < rows).astype(jnp.int32)), width)
+    below = (at_x - 1) * size_y + at_y + jnp.arange(-1, 2)
+    below = jnp.clip(below, 0, size_x * size_y - 1)
+    _, begins = window_of(used_by[below], width)
+    begins = jnp.concatenate([begins, jnp.zeros((6,), jnp.int32)])
     edge = jnp.take(own, border, axis=0, mode="clip")
-    below, above = shift(edge, "gx")
-    line = jnp.stack([below, edge, above])
-    low, high = shift(line, "gy")
-    return own, line, low, high
+    upper = lax.dynamic_slice_in_dim(edge, start, part, axis=0)
+    pair = jnp.stack(shift(upper, edge[:part], "gx"))
+    low, high = shift(edge, edge, "gy")
+    low_pair, high_pair = shift(pair, pair, "gy")
+    return begins, own, edge, low, high, pair, low_pair, high_pair
 
 
 def step(features, pre_norm, out_grad, weight, gamma, beta, neighbors, boundary, counts):
@@ -295,7 +326,6 @@
     rows, chans = feat.shape
     border = boundary[0, 0]
     links = neighbors[0, 0]
-    offsets = links.shape[0]
     width = border.shape[0]
     tiles = -(-rows // TILE)
     plan = plan_segments(links, rows, width, tiles)
@@ -308,9 +338,11 @@
             jnp.sum(zlive, axis=0),
             jnp.sum(zlive * zval, axis=0),
             jnp.broadcast_to(counts[0, 0].astype(F32), (chans,)),
+            jnp.broadcast_to(jnp.sum((border < rows).astype(F32)), (chans,)),
         ]
     )
-    sums = everyone_sum(own)
+    every = from_everyone(own)
+    sums = jnp.sum(every, axis=0)
     count = sums[2]
     mean = sums[0] / count
     var = sums[1] / count - mean * mean
@@ -322,16 +354,15 @@
         live, out_grad[0, 0].astype(F32) * sig * (1.0 + act * (1.0 - sig)), F32(0.0)
     )
     pair = jnp.stack([jnp.sum(grad_act, axis=0), jnp.sum(grad_act * zhat, axis=0)])
-    grads = everyone_sum(pair)
+    grads = jnp.sum(from_everyone(pair), axis=0)
     beta_grad, gamma_grad = grads[0], grads[1]
     dz = jnp.where(
         live,
         gamma * rstd * (grad_act - beta_grad / count - zhat * gamma_grad / count),
         F32(0.0),
     ).astype(BF)
-    pieces = table_pieces(dz, border)
-    near = gather_all(plan, offsets, pieces)
-    wgrad = outer_products(turned, near)
+    pieces = table_pieces(dz, border, every[:, 3, 0].astype(jnp.int32))
+    near, wgrad = gather_outer(plan, pieces, feat, turned)
     weight_grad = scatter_sum(wgrad)
     cut = rows // 8 * 5
     in_grad = [back_products(near, weight, 0, cut)]

time: 181 us -> 163 us (0.901)
  waiting for transfers between devices: 42.4 us -> 25.5 us
  Pallas kernels: 64.4 us -> 57.6 us
  other arithmetic: 18.4 us -> 21.8 us
    ppermute x4 -> x6, waiting for transfers between devices: 13.1 us -> 2.4 us  [shift(): return (lax.ppermute(up, axis, forward), lax.ppermute(down, axis, backward))]
    pallas_call x2 -> x1, Pallas kernels: 45 us -> 38.1 us  [gather_outer(): pl.pallas_call(functools.partial(gather_kernel, rows, width), grid=(group...]
    ppermute x9, waiting for transfers between devices: 19.4 us -> 16.2 us  [halve(): got = lax.ppermute(give, axis, [(i, i ^ 1 << bit) for i in range(count)])]
    all_to_all x2, waiting for transfers between devices: 9.84 us -> 6.91 us  [from_everyone(): return lax.all_to_all(spread, AXES, 0, 0, tiled=True)]
    unnamed x49 -> x56, local copies, waits for them, and re-layouts: 3.4 us -> 0.97 us
    ppermute x9, starting transfers between devices: 19.3 us -> 16.9 us  [halve(): got = lax.ppermute(give, axis, [(i, i ^ 1 << bit) for i in range(count)])]
    all_to_all x2, starting transfers between devices: 9.9 us -> 12.1 us  [from_everyone(): return lax.all_to_all(spread, AXES, 0, 0, tiled=True)]
    reduce_sum x2 -> x4, other arithmetic: 0.09 us -> 2.03 us  [the longest x1 1.3 us: step(): jnp.sum((border < rows).astype(F32))]
  transfers between devices with their start and end apart: 15 -> 17, of which waited for: 10 -> 9; matrix products, arithmetic and copies ran while one was open for 7% -> 10% of each run, Pallas kernels for 11% -> 12%
where the time goes in v3:
time: 163 us; the launch traced here: 162 us
  Pallas kernels  57.6 us (35%)
  starting transfers between devices  39.4 us (24%)
  waiting for transfers between devices  25.5 us (16%)
  other arithmetic  21.8 us (13%)
  local copies, waits for them, and re-layouts  14.9 us (9%)
  between operations  2.65 us (2%)
    pallas_call x1, Pallas kernels, gather_outer(): pl.pallas_call(functools.partial(gather_kernel, rows, width), grid=(group...  38.1 us
    pallas_call x2, Pallas kernels, back_products(): pl.pallas_call(back_kernel, grid=(count // block,), out_shape=jax.ShapeDt...  19.4 us
    ppermute x9, starting transfers between devices, halve(): got = lax.ppermute(give, axis, [(i, i ^ 1 << bit) for i in range(count)])  16.9 us
    ppermute x9, waiting for transfers between devices, halve(): got = lax.ppermute(give, axis, [(i, i ^ 1 << bit) for i in range(count)])  16.2 us
    all_to_all x2, starting transfers between devices, from_everyone(): return lax.all_to_all(spread, AXES, 0, 0, tiled=True)  12.1 us
    ppermute x6, starting transfers between devices, shift(): return (lax.ppermute(up, axis, forward), lax.ppermute(down, axis, backward))  10.4 us
    all_to_all x2, waiting for transfers between devices, from_everyone(): return lax.all_to_all(spread, AXES, 0, 0, tiled=True)  6.91 us
    convert_element_type x9, local copies, waits for them, and re-layouts, halve(): lax.dynamic_index_in_dim(arr, 1 - mine, dim, keepdims=False).astype(BF)  3.85 us
  transfers between devices with their start and end apart: 17, of which 9 were waited for; matrix products, arithmetic and copies ran while one was open for 10% of the time, Pallas kernels for 12%

profile of v3, /device:TPU:0, one launch (start us, length us, event | category | flops | bytes accessed | tf_op | source)
XLA Modules:
  0.0 161.8 jit_solution(12174117547155119247)
XLA Ops:
  5.8 7.3 %all-to-all-start = ((f32[32,4,256]{2,1,0:T(4,128)}), f32[32,4,256]{2,1,0:T(4,128)S(1)}, u32[]{:S(2)}, u32[]{:S(2)}) async-start(f32[32,4,256]{2,1,0:T(4,128)} %broadcast_in_dim.116), calls=%async_computation | async-start | bytes 262144 | tf_op jit(solution)/shard_map/all_to_all | solution.py:25
  14.7 3.4 %select_reduce_fusion.12 = (s32[9,12]{1,0:T(8,128)S(1)}, s32[9,12]{1,0:T(8,128)S(1)}, s32[9,12]{1,0:T(8,128)S(1)}, s32[9,12]{1,0:T(8,128)S(1)}, s32[9,12]{1,0:T(...) fusion(s32[9,3,12,176]{3,2,1,0:T(8,128)S(1)} %reshape.1278), kind=kLoop, calls=%fused_computation.57 | loop fusion | flops 3989520 | bytes 236736 | tf_op jit(solution)/shard_map/reduce_max | solution.py:86
  21.4 2.4 %fusion.42 = (f32[256]{0:T(256)S(1)}, f32[256]{0:T(256)S(1)}, f32[2048,256]{1,0:T(8,128)}) fusion(f32[256]{0:T(256)S(1)} %bitcast.127, f32[256]{0:T(256)S(1)} %bitcast.129, bf16[1,1,2048,256]{3,2,1,0:T(8,128)(2,1)S(1)} %copy-done.1, f32[256]{0:T(256)S(1)} %copy-done.14, f32[256]{0:T(256)S(1)} %copy-done.12, bf16[1,1,2048,256]{3,2,1,0:T(8,128)(2,1)S(1)} %copy-done.6, ...), kind=kLoop, calls=%fused_computation.158 | loop fusion | flops 9436672 | bytes 4202496 | tf_op jit(solution)/shard_map/reduce_sum | solution.py:356
  24.5 4.8 %all-to-all-start.1 = ((f32[32,2,256]{2,1,0:T(2,128)}), f32[32,2,256]{2,1,0:T(2,128)S(1)}, u32[]{:S(2)}, u32[]{:S(2)}) async-start(f32[32,2,256]{2,1,0:T(2,128)} %broadcast_in_dim.117), calls=%async_computation.1 | async-start | bytes 131072 | tf_op jit(solution)/shard_map/all_to_all | solution.py:25
  30.9 5.8 %all-to-all-done.1 = f32[32,2,256]{2,1,0:T(2,128)S(1)} async-done(((f32[32,2,256]{2,1,0:T(2,128)}), f32[32,2,256]{2,1,0:T(2,128)S(1)}, u32[]{:S(2)}, u32[]{:S(2)}) %all-to-all-start.1) | async-done | bytes 65568 | tf_op jit(solution)/shard_map/all_to_all | solution.py:25
  37.3 2.0 %fusion.20.own_ref = bf16[2048,256]{1,0:T(8,128)(2,1)S(1)} fusion(f32[2048,256]{1,0:T(8,128)} %get-tuple-element.34, bf16[1,1,2048,256]{3,2,1,0:T(8,128)(2,1)S(1)} %copy-done.1, f32[256]{0:T(256)S(1)} %bitcast.126, f32[256]{0:T(256)S(1)} %bitcast.135, f32[256]{0:T(256)S(1)} %bitcast.137, f32[256]{0:T(256)S(1)} %bitcast.128, f32[256]{0:T(256)S(1)} %bitcast.130, ...), kind=kLoop, calls=%fused_computation.28 | loop fusion | flops 5242880 | bytes 4202496 | tf_op jit(solution)/shard_map/convert_element_type | solution.py:363
  39.3 2.8 %gather_fusion.1 = bf16[704,256]{1,0:T(8,128)(2,1)S(1)} fusion(bf16[2048,256]{1,0:T(8,128)(2,1)S(1)} %fusion.20.own_ref, s32[1024]{0:T(1024)S(1)} %pad_clamp_fusion), kind=kCustom, calls=%fused_computation.1 | custom fusion | bytes 723712 | tf_op jit(solution)/shard_map/jit(_take)/gather | solution.py:316
  42.2 2.6 %collective-permute-start.2 = (bf16[352,256]{1,0:T(8,128)(2,1)S(1)}, bf16[352,256]{1,0:T(8,128)(2,1)S(1)}, u32[]{:S(2)}, u32[]{:S(2)}) collective-permute-start(bf16[352,256]{1,0:T(8,128)(2,1)S(1)} %get-tuple-element.39), channel_id=1, source_target_pairs={{0,4},{4,8},{8,12},{12,16},{16,20},{20,24},{24,28},{1,5},{5,9},{9,... | collective-permute-start | bytes 540680 | tf_op jit(solution)/shard_map/ppermute | solution.py:32
  46.9 2.4 %collective-permute-start = (bf16[704,256]{1,0:T(8,128)(2,1)S(1)}, bf16[704,256]{1,0:T(8,128)(2,1)}, u32[]{:S(2)}, u32[]{:S(2)}) collective-permute-start(bf16[704,256]{1,0:T(8,128)(2,1)S(1)} %gather_fusion.1), channel_id=1, source_target_pairs={{0,1},{1,2},{2,3},{4,5},{5,6},{6,7},{8,9},{9,10},{10,11},{12,13},{... | collective-permute-start | bytes 1081352 | tf_op jit(solution)/shard_map/ppermute | solution.py:32
  50.6 2.2 %collective-permute-done.2 = bf16[352,256]{1,0:T(8,128)(2,1)S(1)} collective-permute-done((bf16[352,256]{1,0:T(8,128)(2,1)S(1)}, bf16[352,256]{1,0:T(8,128)(2,1)S(1)}, u32[]{:S(2)}, u32[]{:S(2)}) %collective-permute-start.2) | collective-permute-done | bytes 180256 | tf_op jit(solution)/shard_map/ppermute | solution.py:32
  61.8 38.1 %shard_map.120 = (bf16[27,2048,256]{2,1,0:T(8,128)(2,1)}, f32[6912,256]{1,0:T(8,128)}) custom-call(s32[32,9,12]{2,1,0:T(8,128)} %broadcast_add_fusion.listed_ref, s32[10,9,12]{2,1,0:T(8,128)} %copy-done.10, s32[10,9,12]{2,1,0:T(8,128)} %copy-done.7, s32[9]{0:T(128)} %concatenate.67.begin_ref, s32[9,8,2112]{2,1,0:T(8,128)} %pad.10.links_ref, ...), custom_call_target="tpu_custom_call" | custom-call | flops 14495514624 | bytes 28311552 | tf_op jit(solution)/shard_map/pallas_call | solution.py:236
  100.0 3.6 %fusion.21 = bf16[2,2,2,2,216,256]{5,4,0,1,3,2:T(8,128)(2,1)} fusion(f32[2,2,2,2,2,216,256]{6,5,4,3,2,1,0:T(8,128)} %bitcast.117, s32[]{:T(128)S(6)} %select_n.210), kind=kLoop, calls=%fused_computation.29 | loop fusion | bytes 3538948 | tf_op jit(solution)/shard_map/convert_element_type | solution.py:38
  103.5 2.8 %collective-permute-start.6 = (bf16[2,2,2,2,216,256]{5,4,0,1,3,2:T(8,128)(2,1)}, bf16[2,2,2,2,216,256]{5,4,0,1,3,2:T(8,128)(2,1)}, u32[]{:S(2)}, u32[]{:S(2)}) collective-permute-start(bf16[2,2,2,2,216,256]{5,4,0,1,3,2:T(8,128)(2,1)} %fusion.21), channel_id=1, source_target_pairs={{0,1},{1,0},{2,3},{3,2},{4,5},{5,4},{6,7},{7,6},{8,9},{9,8},{10,11... | collective-permute-start | bytes 5308424 | tf_op jit(solution)/shard_map/ppermute | solution.py:39
  106.3 11.4 %shard_map.121 = bf16[1280,256]{1,0:T(8,128)(2,1)} custom-call(bf16[27,2048,256]{2,1,0:T(8,128)(2,1)} %get-tuple-element.6.got_ref, bf16[27,256,256]{2,1,0:T(8,128)(2,1)} %w_ref.3), custom_call_target="tpu_custom_call" | custom-call | flops 4529848320 | bytes 17694720 | tf_op jit(solution)/shard_map/pallas_call | solution.py:284
  117.7 2.0 %bitcast_add_fusion = f32[2,2,2,2,216,256]{5,4,0,1,3,2:T(8,128)S(1)} fusion(bf16[2,2,2,2,216,256]{5,4,0,1,3,2:T(8,128)(2,1)} %collective-permute-done.6, f32[2,2,2,2,2,216,256]{6,5,4,3,2,1,0:T(8,128)S(1)} %bitcast.120, s32[]{:T(128)S(6)} %select_n.209), kind=kLoop, calls=%fused_computation.3 | loop fusion | flops 1769472 | bytes 8847364 | tf_op jit(solution)/shard_map/add | solution.py:41
  120.1 1.8 %collective-permute-start.7 = (bf16[2,2,2,216,128]{4,3,0,1,2:T(8,128)(2,1)S(1)}, bf16[2,2,2,216,128]{4,3,0,1,2:T(8,128)(2,1)S(1)}, u32[]{:S(2)}, u32[]{:S(2)}) collective-permute-start(bf16[2,2,2,216,128]{4,3,0,1,2:T(8,128)(2,1)S(1)} %fusion.23), channel_id=1, source_target_pairs={{0,2},{1,3},{2,0},{3,1},{4,6},{5,7},{6,4},{7,5},{8,10},{9,11},{10,... | collective-permute-start | bytes 1327112 | tf_op jit(solution)/shard_map/ppermute | solution.py:39
  121.9 8.0 %shard_map.122 = bf16[768,256]{1,0:T(8,128)(2,1)} custom-call(bf16[27,2048,256]{2,1,0:T(8,128)(2,1)} %get-tuple-element.6.got_ref, bf16[27,256,256]{2,1,0:T(8,128)(2,1)} %w_ref.3), custom_call_target="tpu_custom_call" | custom-call | flops 2717908992 | bytes 10616832 | tf_op jit(solution)/shard_map/pallas_call | solution.py:284
  131.4 2.0 %maximum_bitcast_fusion = bf16[1,1,2048,256]{3,2,1,0:T(8,128)(2,1)} fusion(bf16[768,256]{1,0:T(8,128)(2,1)} %shard_map.122, bf16[1280,256]{1,0:T(8,128)(2,1)S(1)} %copy-done.2), kind=kLoop, calls=%fused_computation.30 | loop fusion | flops 2097152 | bytes 2097152 | tf_op jit(solution)/shard_map/broadcast_in_dim | solution.py:371
  134.3 8.8 %collective-permute-done.11 = bf16[2,2,2,216,128]{4,3,0,1,2:T(8,128)(2,1)S(1)} collective-permute-done((bf16[2,2,2,216,128]{4,3,0,1,2:T(8,128)(2,1)S(1)}, bf16[2,2,2,216,128]{4,3,0,1,2:T(8,128)(2,1)S(1)}, u32[]{:S(2)}, u32[]{:S(2)}) %collective-permute-start.11) | collective-permute-done | bytes 442400 | tf_op jit(solution)/shard_map/ppermute | solution.py:39
  143.6 3.5 %collective-permute-done.8 = bf16[2,2,216,128]{3,2,0,1:T(8,128)(2,1)S(1)} collective-permute-done((bf16[2,2,216,128]{3,2,0,1:T(8,128)(2,1)S(1)}, bf16[2,2,216,128]{3,2,0,1:T(8,128)(2,1)S(1)}, u32[]{:S(2)}, u32[]{:S(2)}) %collective-permute-start.8) | collective-permute-done | bytes 221216 | tf_op jit(solution)/shard_map/ppermute | solution.py:39
  147.2 3.1 %collective-permute-start.9 = (bf16[2,216,128]{2,1,0:T(8,128)(2,1)S(1)}, bf16[2,216,128]{2,1,0:T(8,128)(2,1)S(1)}, u32[]{:S(2)}, u32[]{:S(2)}) collective-permute-start(bf16[2,216,128]{2,1,0:T(8,128)(2,1)S(1)} %fusion.27), channel_id=1, source_target_pairs={{0,8},{4,12},{8,0},{12,4},{16,24},{20,28},{24,16},{28,20},{1,9},{5... | collective-permute-start | bytes 331784 | tf_op jit(solution)/shard_map/ppermute | solution.py:39
  150.3 2.1 %collective-permute-start.13 = (bf16[2,216,128]{2,1,0:T(8,128)(2,1)S(1)}, bf16[2,216,128]{2,1,0:T(8,128)(2,1)S(1)}, u32[]{:S(2)}, u32[]{:S(2)}) collective-permute-start(bf16[2,216,128]{2,1,0:T(8,128)(2,1)S(1)} %fusion.28), channel_id=1, source_target_pairs={{0,8},{4,12},{8,0},{12,4},{16,24},{20,28},{24,16},{28,20},{1,9},{5... | collective-permute-start | bytes 331784 | tf_op jit(solution)/shard_map/ppermute | solution.py:39
  153.9 2.0 %collective-permute-start.10 = (bf16[216,128]{1,0:T(8,128)(2,1)S(1)}, bf16[216,128]{1,0:T(8,128)(2,1)S(1)}, u32[]{:S(2)}, u32[]{:S(2)}) collective-permute-start(bf16[216,128]{1,0:T(8,128)(2,1)S(1)} %fusion.36), channel_id=1, source_target_pairs={{0,16},{4,20},{8,24},{12,28},{16,0},{20,4},{24,8},{28,12},{1,17},{... | collective-permute-start | bytes 165896 | tf_op jit(solution)/shard_map/ppermute | solution.py:39
  156.0 2.7 %collective-permute-start.14 = (bf16[216,128]{1,0:T(8,128)(2,1)S(1)}, bf16[216,128]{1,0:T(8,128)(2,1)S(1)}, u32[]{:S(2)}, u32[]{:S(2)}) collective-permute-start(bf16[216,128]{1,0:T(8,128)(2,1)S(1)} %fusion.37), channel_id=1, source_target_pairs={{0,16},{4,20},{8,24},{12,28},{16,0},{20,4},{24,8},{28,12},{1,17},{... | collective-permute-start | bytes 165896 | tf_op jit(solution)/shard_map/ppermute | solution.py:39
  (134 shorter events, 31.7 us)
Async XLA Ops:
  5.0 13.7 %copy-start.11 = (s32[1,1,704]{2,1,0:T(1,128)S(1)}, s32[1,1,704]{2,1,0:T(1,128)}, u32[]{:S(2)}) copy-start(s32[1,1,704]{2,1,0:T(1,128)} %param.16) | copy-start | bytes 8452
  5.8 15.5 %all-to-all-start = ((f32[32,4,256]{2,1,0:T(4,128)}), f32[32,4,256]{2,1,0:T(4,128)S(1)}, u32[]{:S(2)}, u32[]{:S(2)}) async-start(f32[32,4,256]{2,1,0:T(4,128)} %broadcast_in_dim.116), calls=%async_computation | async-start | bytes 262144 | tf_op jit(solution)/shard_map/all_to_all | solution.py:25
  13.1 8.3 %copy-start.1 = (bf16[1,1,2048,256]{3,2,1,0:T(8,128)(2,1)S(1)}, bf16[1,1,2048,256]{3,2,1,0:T(8,128)(2,1)}, u32[]{:S(2)}) copy-start(bf16[1,1,2048,256]{3,2,1,0:T(8,128)(2,1)} %param.10) | copy-start | bytes 3145732
  24.5 12.2 %all-to-all-start.1 = ((f32[32,2,256]{2,1,0:T(2,128)}), f32[32,2,256]{2,1,0:T(2,128)S(1)}, u32[]{:S(2)}, u32[]{:S(2)}) async-start(f32[32,2,256]{2,1,0:T(2,128)} %broadcast_in_dim.117), calls=%async_computation.1 | async-start | bytes 131072 | tf_op jit(solution)/shard_map/all_to_all | solution.py:25
  42.1 16.1 %copy-start.3 = (bf16[704,256]{1,0:T(8,128)(2,1)}, bf16[704,256]{1,0:T(8,128)(2,1)S(1)}, u32[]{:S(2)}) copy-start(bf16[704,256]{1,0:T(8,128)(2,1)S(1)} %gather_fusion.1) | copy-start | bytes 1081348
  42.2 14.7 %copy-start.4 = (bf16[1,1,2048,256]{3,2,1,0:T(8,128)(2,1)S(1)}, bf16[1,1,2048,256]{3,2,1,0:T(8,128)(2,1)}, u32[]{:S(2)}) copy-start(bf16[1,1,2048,256]{3,2,1,0:T(8,128)(2,1)} %param.9) | copy-start | bytes 3145732
  42.2 10.5 %collective-permute-start.2 = (bf16[352,256]{1,0:T(8,128)(2,1)S(1)}, bf16[352,256]{1,0:T(8,128)(2,1)S(1)}, u32[]{:S(2)}, u32[]{:S(2)}) collective-permute-start(bf16[352,256]{1,0:T(8,128)(2,1)S(1)} %get-tuple-element.39), channel_id=1, source_target_pairs={{0,4},{4,8},{8,12},{12,16},{16,20},{20,24},{24,28},{1,5},{5,9},{9,... | collective-permute-start | bytes 540680 | tf_op jit(solution)/shard_map/ppermute | solution.py:32
  44.9 8.1 %collective-permute-start.3 = (bf16[352,256]{1,0:T(8,128)(2,1)S(1)}, bf16[352,256]{1,0:T(8,128)(2,1)S(1)}, u32[]{:S(2)}, u32[]{:S(2)}) collective-permute-start(bf16[352,256]{1,0:T(8,128)(2,1)S(1)} %get-tuple-element.40), channel_id=1, source_target_pairs={{4,0},{8,4},{12,8},{16,12},{20,16},{24,20},{28,24},{5,1},{9,5},{13... | collective-permute-start | bytes 540680 | tf_op jit(solution)/shard_map/ppermute | solution.py:32
  46.9 14.0 %collective-permute-start = (bf16[704,256]{1,0:T(8,128)(2,1)S(1)}, bf16[704,256]{1,0:T(8,128)(2,1)}, u32[]{:S(2)}, u32[]{:S(2)}) collective-permute-start(bf16[704,256]{1,0:T(8,128)(2,1)S(1)} %gather_fusion.1), channel_id=1, source_target_pairs={{0,1},{1,2},{2,3},{4,5},{5,6},{6,7},{8,9},{9,10},{10,11},{12,13},{... | collective-permute-start | bytes 1081352 | tf_op jit(solution)/shard_map/ppermute | solution.py:32
  49.3 11.6 %collective-permute-start.1 = (bf16[704,256]{1,0:T(8,128)(2,1)S(1)}, bf16[704,256]{1,0:T(8,128)(2,1)S(1)}, u32[]{:S(2)}, u32[]{:S(2)}) collective-permute-start(bf16[704,256]{1,0:T(8,128)(2,1)S(1)} %gather_fusion.1), channel_id=1, source_target_pairs={{1,0},{2,1},{3,2},{5,4},{6,5},{7,6},{9,8},{10,9},{11,10},{13,12},{... | collective-permute-start | bytes 1081352 | tf_op jit(solution)/shard_map/ppermute | solution.py:32
  53.0 7.9 %collective-permute-start.4 = (bf16[2,352,256]{2,1,0:T(8,128)(2,1)S(1)}, bf16[2,352,256]{2,1,0:T(8,128)(2,1)S(1)}, u32[]{:S(2)}, u32[]{:S(2)}) collective-permute-start(bf16[2,352,256]{2,1,0:T(8,128)(2,1)S(1)} %pad_maximum_fusion.pair_ref), channel_id=1, source_target_pairs={{0,1},{1,2},{2,3},{4,5},{5,6},{6,7},{8,9},{9,10},{10,11},{12,13},{... | collective-permute-start | bytes 1081352 | tf_op jit(solution)/shard_map/ppermute | solution.py:32
  54.3 6.6 %collective-permute-start.5 = (bf16[2,352,256]{2,1,0:T(8,128)(2,1)S(1)}, bf16[2,352,256]{2,1,0:T(8,128)(2,1)}, u32[]{:S(2)}, u32[]{:S(2)}) collective-permute-start(bf16[2,352,256]{2,1,0:T(8,128)(2,1)S(1)} %pad_maximum_fusion.pair_ref), channel_id=1, source_target_pairs={{1,0},{2,1},{3,2},{5,4},{6,5},{7,6},{9,8},{10,9},{11,10},{13,12},{... | collective-permute-start | bytes 1081352 | tf_op jit(solution)/shard_map/ppermute | solution.py:32
  100.0 17.7 %slice-start = ((s8[7077888]{0:T(1024)(128)(4,1)}), s8[2883584]{0:T(1024)(128)(4,1)S(1)}, s32[]{:S(2)}) async-start(s8[7077888]{0:T(1024)(128)(4,1)} %bitcast.118), calls=%async_computation.2 | async-start | bytes 5767168
  103.5 14.2 %collective-permute-start.6 = (bf16[2,2,2,2,216,256]{5,4,0,1,3,2:T(8,128)(2,1)}, bf16[2,2,2,2,216,256]{5,4,0,1,3,2:T(8,128)(2,1)}, u32[]{:S(2)}, u32[]{:S(2)}) collective-permute-start(bf16[2,2,2,2,216,256]{5,4,0,1,3,2:T(8,128)(2,1)} %fusion.21), channel_id=1, source_target_pairs={{0,1},{1,0},{2,3},{3,2},{4,5},{5,4},{6,7},{7,6},{8,9},{9,8},{10,11... | collective-permute-start | bytes 5308424 | tf_op jit(solution)/shard_map/ppermute | solution.py:39
  106.3 11.4 %slice-start.1 = ((s8[7077888]{0:T(1024)(128)(4,1)}), s8[4194304]{0:T(1024)(128)(4,1)S(1)}, s32[]{:S(2)}) async-start(s8[7077888]{0:T(1024)(128)(4,1)} %bitcast.118), calls=%async_computation.3 | async-start | bytes 8388608
  120.1 11.3 %copy-start.2 = (bf16[1280,256]{1,0:T(8,128)(2,1)S(1)}, bf16[1280,256]{1,0:T(8,128)(2,1)}, u32[]{:S(2)}) copy-start(bf16[1280,256]{1,0:T(8,128)(2,1)} %shard_map.121) | copy-start | bytes 1966084
  120.1 13.3 %collective-permute-start.7 = (bf16[2,2,2,216,128]{4,3,0,1,2:T(8,128)(2,1)S(1)}, bf16[2,2,2,216,128]{4,3,0,1,2:T(8,128)(2,1)S(1)}, u32[]{:S(2)}, u32[]{:S(2)}) collective-permute-start(bf16[2,2,2,216,128]{4,3,0,1,2:T(8,128)(2,1)S(1)} %fusion.23), channel_id=1, source_target_pairs={{0,2},{1,3},{2,0},{3,1},{4,6},{5,7},{6,4},{7,5},{8,10},{9,11},{10,... | collective-permute-start | bytes 1327112 | tf_op jit(solution)/shard_map/ppermute | solution.py:39
  130.0 13.1 %collective-permute-start.11 = (bf16[2,2,2,216,128]{4,3,0,1,2:T(8,128)(2,1)S(1)}, bf16[2,2,2,216,128]{4,3,0,1,2:T(8,128)(2,1)S(1)}, u32[]{:S(2)}, u32[]{:S(2)}) collective-permute-start(bf16[2,2,2,216,128]{4,3,0,1,2:T(8,128)(2,1)S(1)} %fusion.24), channel_id=1, source_target_pairs={{0,4},{4,0},{8,12},{12,8},{16,20},{20,16},{24,28},{28,24},{1,5},{5... | collective-permute-start | bytes 1327112 | tf_op jit(solution)/shard_map/ppermute | solution.py:39
  133.5 13.5 %collective-permute-start.8 = (bf16[2,2,216,128]{3,2,0,1:T(8,128)(2,1)S(1)}, bf16[2,2,216,128]{3,2,0,1:T(8,128)(2,1)S(1)}, u32[]{:S(2)}, u32[]{:S(2)}) collective-permute-start(bf16[2,2,216,128]{3,2,0,1:T(8,128)(2,1)S(1)} %fusion.25), channel_id=1, source_target_pairs={{0,4},{4,0},{8,12},{12,8},{16,20},{20,16},{24,28},{28,24},{1,5},{5... | collective-permute-start | bytes 663560 | tf_op jit(solution)/shard_map/ppermute | solution.py:39
  143.2 7.0 %collective-permute-start.12 = (bf16[2,2,216,128]{3,2,0,1:T(8,128)(2,1)S(1)}, bf16[2,2,216,128]{3,2,0,1:T(8,128)(2,1)S(1)}, u32[]{:S(2)}, u32[]{:S(2)}) collective-permute-start(bf16[2,2,216,128]{3,2,0,1:T(8,128)(2,1)S(1)} %fusion.26), channel_id=1, source_target_pairs={{0,2},{1,3},{2,0},{3,1},{4,6},{5,7},{6,4},{7,5},{8,10},{9,11},{10,... | collective-permute-start | bytes 663560 | tf_op jit(solution)/shard_map/ppermute | solution.py:39
  147.2 6.7 %collective-permute-start.9 = (bf16[2,216,128]{2,1,0:T(8,128)(2,1)S(1)}, bf16[2,216,128]{2,1,0:T(8,128)(2,1)S(1)}, u32[]{:S(2)}, u32[]{:S(2)}) collective-permute-start(bf16[2,216,128]{2,1,0:T(8,128)(2,1)S(1)} %fusion.27), channel_id=1, source_target_pairs={{0,8},{4,12},{8,0},{12,4},{16,24},{20,28},{24,16},{28,20},{1,9},{5... | collective-permute-start | bytes 331784 | tf_op jit(solution)/shard_map/ppermute | solution.py:39
  150.3 5.6 %collective-permute-start.13 = (bf16[2,216,128]{2,1,0:T(8,128)(2,1)S(1)}, bf16[2,216,128]{2,1,0:T(8,128)(2,1)S(1)}, u32[]{:S(2)}, u32[]{:S(2)}) collective-permute-start(bf16[2,216,128]{2,1,0:T(8,128)(2,1)S(1)} %fusion.28), channel_id=1, source_target_pairs={{0,8},{4,12},{8,0},{12,4},{16,24},{20,28},{24,16},{28,20},{1,9},{5... | collective-permute-start | bytes 331784 | tf_op jit(solution)/shard_map/ppermute | solution.py:39
  153.9 5.9 %collective-permute-start.10 = (bf16[216,128]{1,0:T(8,128)(2,1)S(1)}, bf16[216,128]{1,0:T(8,128)(2,1)S(1)}, u32[]{:S(2)}, u32[]{:S(2)}) collective-permute-start(bf16[216,128]{1,0:T(8,128)(2,1)S(1)} %fusion.36), channel_id=1, source_target_pairs={{0,16},{4,20},{8,24},{12,28},{16,0},{20,4},{24,8},{28,12},{1,17},{... | collective-permute-start | bytes 165896 | tf_op jit(solution)/shard_map/ppermute | solution.py:39
  156.0 5.1 %collective-permute-start.14 = (bf16[216,128]{1,0:T(8,128)(2,1)S(1)}, bf16[216,128]{1,0:T(8,128)(2,1)S(1)}, u32[]{:S(2)}, u32[]{:S(2)}) collective-permute-start(bf16[216,128]{1,0:T(8,128)(2,1)S(1)} %fusion.37), channel_id=1, source_target_pairs={{0,16},{4,20},{8,24},{12,28},{16,0},{20,4},{24,8},{28,12},{1,17},{... | collective-permute-start | bytes 165896 | tf_op jit(solution)/shard_map/ppermute | solution.py:39
  (12 other events, 63.9 us)

commit v4 on v3

--- a/solution.py
+++ b/solution.py
@@ -12,6 +12,7 @@
 SEG = 16
 LANES = 128
 SEGS = 16
+PARTS = 9
 LISTED = 2
 NOWHERE = -(1 << 20)
 BF = jnp.bfloat16
@@ -169,23 +170,30 @@
             jnp.concatenate(hot, axis=1), source, preferred_element_type=F32
         ).astype(BF)
 
-    upright = jnp.transpose(links_ref[0])
+    groups = links_ref.shape[0]
+    slot = lax.rem(group, 2)
+
+    @pl.when(group == 0)
+    def _():
+        columns[0] = jnp.transpose(links_ref[0])
+
     most = jnp.int32(0)
     for tile in range(tiles):
-        start, stop = tile * TILE, min((tile + 1) * TILE, rows)
-        names, source = source_of([listed_ref[j, group, tile] for j in range(SEGS)])
-        for z in range(3):
-            got_ref[2 - z, start:stop] = pick(upright[start:stop, z : z + 1], names, source)
         most = jnp.maximum(most, end_ref[9, group, tile])
     for z in range(3):
-        wg_ref[z * chans : (z + 1) * chans] = jnp.dot(
-            turned_ref[...], got_ref[z], preferred_element_type=F32
+        for tile in range(tiles):
+            start, stop = tile * TILE, min((tile + 1) * TILE, rows)
+            names, source = source_of([listed_ref[j, group, tile] for j in range(SEGS)])
+            col = columns[slot, start:stop, z : z + 1]
+            got_ref[2 - z, start:stop] = pick(col, names, source)
+        if z == 2:
+            columns[1 - slot] = jnp.transpose(links_ref[jnp.minimum(group + 1, groups - 1)])
+        wg_ref[(2 - z) * chans : (3 - z) * chans] = jnp.dot(
+            turned_ref[...], got_ref[2 - z], preferred_element_type=F32
         )
 
     @pl.when(most > SEGS)
     def _():
-        columns[...] = upright
-
         @pl.loop(0, tiles)
         def _(tile):
             count = (end_ref[9, group, tile] + SEGS - 1) // SEGS
@@ -218,7 +226,7 @@
                 names, source = source_of([spill[j] for j in range(SEGS)])
                 beside = feat_ref[pl.ds(start, TILE), :]
                 for z in range(3):
-                    col = columns[pl.ds(start, TILE), z : z + 1]
+                    col = columns[slot, pl.ds(start, TILE), z : z + 1]
                     more = pick(jnp.where(fresh, col, NOWHERE), names, source)
                     got_ref[2 - z, pl.ds(start, TILE)] += more
                     wg_ref[(2 - z) * chans : (3 - z) * chans] += lax.dot_general(
@@ -241,7 +249,7 @@
             jax.ShapeDtypeStruct((3 * groups * chans, chans), F32),
         ),
         in_specs=[smem] * 4
-        + [pl.BlockSpec((1,) + laid.shape[1:], lambda g: (g, 0, 0))]
+        + [pl.BlockSpec(laid.shape, lambda g: (0, 0, 0))]
         + [pl.BlockSpec(memory_space=pl.ANY)] * 7
         + [
             pl.BlockSpec((chans, rows), lambda g: (0, 0)),
@@ -253,7 +261,7 @@
         ),
         scratch_shapes=[
             pltpu.VMEM((rows + 9 * width, chans), BF),
-            pltpu.VMEM((laid.shape[2], laid.shape[1]), jnp.int32),
+            pltpu.VMEM((2, laid.shape[2], laid.shape[1]), jnp.int32),
             pltpu.SMEM((SEGS,), jnp.int32),
             pltpu.SemaphoreType.DMA((10,)),
         ],
@@ -266,11 +274,12 @@
     )(listed, low, ends, begins, laid, *pieces, turned, feat)
 
 
-def back_kernel(got_ref, w_ref, out_ref):
-    offsets = w_ref.shape[0]
+def back_kernel(*refs):
+    gots, w_ref, out_ref = refs[:-2], refs[-2], refs[-1]
+    got = [ref[k] for ref in gots for k in range(ref.shape[0])]
     total = lax.dot_general(
-        jnp.concatenate([got_ref[k] for k in range(offsets)], axis=1),
-        jnp.concatenate([w_ref[k] for k in range(offsets)], axis=1),
+        jnp.concatenate(got, axis=1),
+        jnp.concatenate([w_ref[k] for k in range(len(got))], axis=1),
         (((1,), (1,)), ((), ())),
         preferred_element_type=F32,
     )
@@ -286,17 +295,21 @@
         grid=(count // block,),
         out_shape=jax.ShapeDtypeStruct((count, chans), BF),
         in_specs=[
-            pl.BlockSpec((offsets, block, chans), lambda i: (0, i + first // block, 0)),
-            pl.BlockSpec(weight.shape, lambda i: (0, 0, 0)),
-        ],
+            pl.BlockSpec(
+                (offsets // PARTS, block, chans),
+                lambda i, part=part: (part, i + first // block, 0),
+            )
+            for part in range(PARTS)
+        ]
+        + [pl.BlockSpec(weight.shape, lambda i: (0, 0, 0))],
         out_specs=pl.BlockSpec((block, chans), lambda i: (i, 0)),
-        compiler_params=pltpu.CompilerParams(vmem_limit_bytes=56 << 20),
+        compiler_params=pltpu.CompilerParams(vmem_limit_bytes=40 << 20),
         cost_estimate=pl.CostEstimate(
             flops=2 * offsets * count * chans * chans,
             bytes_accessed=2 * offsets * count * chans,
             transcendentals=0,
         ),
-    )(got, weight)
+    )(*[got] * PARTS, weight)
 
 
 def window_of(used, width):
@@ -364,7 +377,7 @@
     pieces = table_pieces(dz, border, every[:, 3, 0].astype(jnp.int32))
     near, wgrad = gather_outer(plan, pieces, feat, turned)
     weight_grad = scatter_sum(wgrad)
-    cut = rows // 8 * 5
+    cut = rows // 4 * 3
     in_grad = [back_products(near, weight, 0, cut)]
     in_grad.append(back_products(near, weight, cut, rows))
     in_grad = jnp.concatenate(in_grad)

time: 163 us -> 154 us (0.945)
  Pallas kernels: 57.6 us -> 49.7 us
    pallas_call x2, Pallas kernels: 19.4 us -> 15.3 us  [back_products(): pl.pallas_call(back_kernel, grid=(count // block,), out_shape=jax.ShapeDt...]
    pallas_call x1, Pallas kernels: 38.1 us -> 34.4 us  [gather_outer(): pl.pallas_call(functools.partial(gather_kernel, rows, width), grid=(group...]
  transfers between devices with their start and end apart: 17 -> 17, of which waited for: 9 -> 11; matrix products, arithmetic and copies ran while one was open for 10% -> 10% of each run, Pallas kernels for 12% -> 10%
where the time goes in v4:
time: 154 us
  Pallas kernels  49.7 us (32%)
  starting transfers between devices  40 us (26%)
  waiting for transfers between devices  25.9 us (17%)
  other arithmetic  20.8 us (14%)
  local copies, waits for them, and re-layouts  14.9 us (10%)
  between operations  2.67 us (2%)
    pallas_call x1, Pallas kernels, gather_outer(): pl.pallas_call(functools.partial(gather_kernel, rows, width), grid=(group...  34.4 us
    ppermute x9, starting transfers between devices, halve(): got = lax.ppermute(give, axis, [(i, i ^ 1 << bit) for i in range(count)])  17.5 us
    ppermute x9, waiting for transfers between devices, halve(): got = lax.ppermute(give, axis, [(i, i ^ 1 << bit) for i in range(count)])  16.6 us
    pallas_call x2, Pallas kernels, back_products(): pl.pallas_call(back_kernel, grid=(count // block,), out_shape=jax.ShapeDt...  15.3 us
    all_to_all x2, starting transfers between devices, from_everyone(): return lax.all_to_all(spread, AXES, 0, 0, tiled=True)  12.1 us
    ppermute x6, starting transfers between devices, shift(): return (lax.ppermute(up, axis, forward), lax.ppermute(down, axis, backward))  10.4 us
    all_to_all x2, waiting for transfers between devices, from_everyone(): return lax.all_to_all(spread, AXES, 0, 0, tiled=True)  6.91 us
    convert_element_type x9, local copies, waits for them, and re-layouts, halve(): lax.dynamic_index_in_dim(arr, 1 - mine, dim, keepdims=False).astype(BF)  3.86 us
  transfers between devices with their start and end apart: 17, of which 11 were waited for; matrix products, arithmetic and copies ran while one was open for 10% of the time, Pallas kernels for 10%

profile of v4, /device:TPU:0, one launch (start us, length us, event | category | flops | bytes accessed | tf_op | source)
XLA Modules:
  0.0 153.9 jit_solution(15969283043144442791)
XLA Ops:
  5.8 7.3 %all-to-all-start = ((f32[32,4,256]{2,1,0:T(4,128)}), f32[32,4,256]{2,1,0:T(4,128)S(1)}, u32[]{:S(2)}, u32[]{:S(2)}) async-start(f32[32,4,256]{2,1,0:T(4,128)} %broadcast_in_dim.116), calls=%async_computation | async-start | bytes 262144 | tf_op jit(solution)/shard_map/all_to_all | solution.py:26
  14.7 3.4 %select_reduce_fusion.12 = (s32[9,12]{1,0:T(8,128)S(1)}, s32[9,12]{1,0:T(8,128)S(1)}, s32[9,12]{1,0:T(8,128)S(1)}, s32[9,12]{1,0:T(8,128)S(1)}, s32[9,12]{1,0:T(...) fusion(s32[9,3,12,176]{3,2,1,0:T(8,128)S(1)} %reshape.1278), kind=kLoop, calls=%fused_computation.57 | loop fusion | flops 3989520 | bytes 236736 | tf_op jit(solution)/shard_map/reduce_max | solution.py:87
  21.4 2.4 %fusion.42 = (f32[256]{0:T(256)S(1)}, f32[256]{0:T(256)S(1)}, f32[2048,256]{1,0:T(8,128)}) fusion(f32[256]{0:T(256)S(1)} %bitcast.125, f32[256]{0:T(256)S(1)} %bitcast.127, bf16[1,1,2048,256]{3,2,1,0:T(8,128)(2,1)S(1)} %copy-done.2, f32[256]{0:T(256)S(1)} %copy-done.15, f32[256]{0:T(256)S(1)} %copy-done.13, bf16[1,1,2048,256]{3,2,1,0:T(8,128)(2,1)S(1)} %copy-done.7, ...), kind=kLoop, calls=%fused_computation.158 | loop fusion | flops 9436672 | bytes 4202496 | tf_op jit(solution)/shard_map/reduce_sum | solution.py:369
  24.5 4.8 %all-to-all-start.1 = ((f32[32,2,256]{2,1,0:T(2,128)}), f32[32,2,256]{2,1,0:T(2,128)S(1)}, u32[]{:S(2)}, u32[]{:S(2)}) async-start(f32[32,2,256]{2,1,0:T(2,128)} %broadcast_in_dim.117), calls=%async_computation.1 | async-start | bytes 131072 | tf_op jit(solution)/shard_map/all_to_all | solution.py:26
  30.9 5.8 %all-to-all-done.1 = f32[32,2,256]{2,1,0:T(2,128)S(1)} async-done(((f32[32,2,256]{2,1,0:T(2,128)}), f32[32,2,256]{2,1,0:T(2,128)S(1)}, u32[]{:S(2)}, u32[]{:S(2)}) %all-to-all-start.1) | async-done | bytes 65568 | tf_op jit(solution)/shard_map/all_to_all | solution.py:26
  37.3 2.0 %fusion.20.own_ref = bf16[2048,256]{1,0:T(8,128)(2,1)S(1)} fusion(f32[2048,256]{1,0:T(8,128)} %get-tuple-element.34, bf16[1,1,2048,256]{3,2,1,0:T(8,128)(2,1)S(1)} %copy-done.2, f32[256]{0:T(256)S(1)} %bitcast.124, f32[256]{0:T(256)S(1)} %bitcast.133, f32[256]{0:T(256)S(1)} %bitcast.135, f32[256]{0:T(256)S(1)} %bitcast.126, f32[256]{0:T(256)S(1)} %bitcast.128, ...), kind=kLoop, calls=%fused_computation.28 | loop fusion | flops 5242880 | bytes 4202496 | tf_op jit(solution)/shard_map/convert_element_type | solution.py:376
  39.3 2.8 %gather_fusion.1 = bf16[704,256]{1,0:T(8,128)(2,1)S(1)} fusion(bf16[2048,256]{1,0:T(8,128)(2,1)S(1)} %fusion.20.own_ref, s32[1024]{0:T(1024)S(1)} %pad_clamp_fusion), kind=kCustom, calls=%fused_computation.1 | custom fusion | bytes 723712 | tf_op jit(solution)/shard_map/jit(_take)/gather | solution.py:329
  42.2 2.6 %collective-permute-start.2 = (bf16[352,256]{1,0:T(8,128)(2,1)S(1)}, bf16[352,256]{1,0:T(8,128)(2,1)S(1)}, u32[]{:S(2)}, u32[]{:S(2)}) collective-permute-start(bf16[352,256]{1,0:T(8,128)(2,1)S(1)} %get-tuple-element.39), channel_id=1, source_target_pairs={{0,4},{4,8},{8,12},{12,16},{16,20},{20,24},{24,28},{1,5},{5,9},{9,... | collective-permute-start | bytes 540680 | tf_op jit(solution)/shard_map/ppermute | solution.py:33
  46.9 2.4 %collective-permute-start = (bf16[704,256]{1,0:T(8,128)(2,1)S(1)}, bf16[704,256]{1,0:T(8,128)(2,1)}, u32[]{:S(2)}, u32[]{:S(2)}) collective-permute-start(bf16[704,256]{1,0:T(8,128)(2,1)S(1)} %gather_fusion.1), channel_id=1, source_target_pairs={{0,1},{1,2},{2,3},{4,5},{5,6},{6,7},{8,9},{9,10},{10,11},{12,13},{... | collective-permute-start | bytes 1081352 | tf_op jit(solution)/shard_map/ppermute | solution.py:33
  50.6 2.2 %collective-permute-done.2 = bf16[352,256]{1,0:T(8,128)(2,1)S(1)} collective-permute-done((bf16[352,256]{1,0:T(8,128)(2,1)S(1)}, bf16[352,256]{1,0:T(8,128)(2,1)S(1)}, u32[]{:S(2)}, u32[]{:S(2)}) %collective-permute-start.2) | collective-permute-done | bytes 180256 | tf_op jit(solution)/shard_map/ppermute | solution.py:33
  61.8 34.4 %shard_map.120 = (bf16[27,2048,256]{2,1,0:T(8,128)(2,1)}, f32[6912,256]{1,0:T(8,128)}) custom-call(s32[32,9,12]{2,1,0:T(8,128)} %broadcast_add_fusion.listed_ref, s32[10,9,12]{2,1,0:T(8,128)} %copy-done.11, s32[10,9,12]{2,1,0:T(8,128)} %copy-done.8, s32[9]{0:T(128)} %concatenate.67.begin_ref, s32[9,8,2112]{2,1,0:T(8,128)} %pad.10.links_ref, ...), custom_call_target="tpu_custom_call" | custom-call | flops 14495514624 | bytes 28311552 | tf_op jit(solution)/shard_map/pallas_call | solution.py:244
  96.2 3.6 %fusion.21 = bf16[2,2,2,2,216,256]{5,4,0,1,3,2:T(8,128)(2,1)} fusion(f32[2,2,2,2,2,216,256]{6,5,4,3,2,1,0:T(8,128)} %bitcast.117, s32[]{:T(128)S(6)} %select_n.210), kind=kLoop, calls=%fused_computation.29 | loop fusion | bytes 3538948 | tf_op jit(solution)/shard_map/convert_element_type | solution.py:39
  99.8 2.8 %collective-permute-start.6 = (bf16[2,2,2,2,216,256]{5,4,0,1,3,2:T(8,128)(2,1)}, bf16[2,2,2,2,216,256]{5,4,0,1,3,2:T(8,128)(2,1)}, u32[]{:S(2)}, u32[]{:S(2)}) collective-permute-start(bf16[2,2,2,2,216,256]{5,4,0,1,3,2:T(8,128)(2,1)} %fusion.21), channel_id=1, source_target_pairs={{0,1},{1,0},{2,3},{3,2},{4,5},{5,4},{6,7},{7,6},{8,9},{9,8},{10,11... | collective-permute-start | bytes 5308424 | tf_op jit(solution)/shard_map/ppermute | solution.py:40
  102.6 11.0 %shard_map.121 = bf16[1536,256]{1,0:T(8,128)(2,1)S(1)} custom-call(bf16[27,2048,256]{2,1,0:T(8,128)(2,1)} %get-tuple-element.6.refs_0_.refs_1_.refs_2_.refs_3_.refs_4_.refs_5_.refs_6_.refs_7_.refs_8_, bf16[27,2048,256]{2,1,0:T(8,128)(2,1)} %get-tuple-element.6.refs_0_.refs_1_.refs_2_.refs_3_.refs_4_.refs_5_.refs_6_.refs_7_.refs_8_, ...), custom_call_target="tpu_custom_call" | custom-call | flops 5435817984 | bytes 21233664 | tf_op jit(solution)/shard_map/pallas_call | solution.py:293
  113.7 1.9 %bitcast_add_fusion = f32[2,2,2,2,216,256]{5,4,0,1,3,2:T(8,128)S(1)} fusion(bf16[2,2,2,2,216,256]{5,4,0,1,3,2:T(8,128)(2,1)} %collective-permute-done.6, f32[2,2,2,2,2,216,256]{6,5,4,3,2,1,0:T(8,128)S(1)} %bitcast.118, s32[]{:T(128)S(6)} %select_n.209), kind=kLoop, calls=%fused_computation.3 | loop fusion | flops 1769472 | bytes 8847364 | tf_op jit(solution)/shard_map/add | solution.py:42
  116.0 1.8 %collective-permute-start.7 = (bf16[2,2,2,216,128]{4,3,0,1,2:T(8,128)(2,1)S(1)}, bf16[2,2,2,216,128]{4,3,0,1,2:T(8,128)(2,1)S(1)}, u32[]{:S(2)}, u32[]{:S(2)}) collective-permute-start(bf16[2,2,2,216,128]{4,3,0,1,2:T(8,128)(2,1)S(1)} %fusion.23), channel_id=1, source_target_pairs={{0,2},{1,3},{2,0},{3,1},{4,6},{5,7},{6,4},{7,5},{8,10},{9,11},{10,... | collective-permute-start | bytes 1327112 | tf_op jit(solution)/shard_map/ppermute | solution.py:40
  117.8 4.2 %shard_map.122 = bf16[512,256]{1,0:T(8,128)(2,1)S(1)} custom-call(bf16[27,2048,256]{2,1,0:T(8,128)(2,1)} %get-tuple-element.6.refs_0_.refs_1_.refs_2_.refs_3_.refs_4_.refs_5_.refs_6_.refs_7_.refs_8_, bf16[27,2048,256]{2,1,0:T(8,128)(2,1)} %get-tuple-element.6.refs_0_.refs_1_.refs_2_.refs_3_.refs_4_.refs_5_.refs_6_.refs_7_.refs_8_, ...), custom_call_target="tpu_custom_call" | custom-call | flops 1811939328 | bytes 7077888 | tf_op jit(solution)/shard_map/pallas_call | solution.py:293
  124.5 4.1 %collective-permute-done.7 = bf16[2,2,2,216,128]{4,3,0,1,2:T(8,128)(2,1)S(1)} collective-permute-done((bf16[2,2,2,216,128]{4,3,0,1,2:T(8,128)(2,1)S(1)}, bf16[2,2,2,216,128]{4,3,0,1,2:T(8,128)(2,1)S(1)}, u32[]{:S(2)}, u32[]{:S(2)}) %collective-permute-start.7) | collective-permute-done | bytes 442400 | tf_op jit(solution)/shard_map/ppermute | solution.py:40
  130.1 5.1 %collective-permute-done.11 = bf16[2,2,2,216,128]{4,3,0,1,2:T(8,128)(2,1)S(1)} collective-permute-done((bf16[2,2,2,216,128]{4,3,0,1,2:T(8,128)(2,1)S(1)}, bf16[2,2,2,216,128]{4,3,0,1,2:T(8,128)(2,1)S(1)}, u32[]{:S(2)}, u32[]{:S(2)}) %collective-permute-start.11) | collective-permute-done | bytes 442400 | tf_op jit(solution)/shard_map/ppermute | solution.py:40
  135.7 3.5 %collective-permute-done.8 = bf16[2,2,216,128]{3,2,0,1:T(8,128)(2,1)S(1)} collective-permute-done((bf16[2,2,216,128]{3,2,0,1:T(8,128)(2,1)S(1)}, bf16[2,2,216,128]{3,2,0,1:T(8,128)(2,1)S(1)}, u32[]{:S(2)}, u32[]{:S(2)}) %collective-permute-start.8) | collective-permute-done | bytes 221216 | tf_op jit(solution)/shard_map/ppermute | solution.py:40
  139.3 3.0 %collective-permute-start.9 = (bf16[2,216,128]{2,1,0:T(8,128)(2,1)S(1)}, bf16[2,216,128]{2,1,0:T(8,128)(2,1)S(1)}, u32[]{:S(2)}, u32[]{:S(2)}) collective-permute-start(bf16[2,216,128]{2,1,0:T(8,128)(2,1)S(1)} %fusion.27), channel_id=1, source_target_pairs={{0,8},{4,12},{8,0},{12,4},{16,24},{20,28},{24,16},{28,20},{1,9},{5... | collective-permute-start | bytes 331784 | tf_op jit(solution)/shard_map/ppermute | solution.py:40
  142.4 2.1 %collective-permute-start.13 = (bf16[2,216,128]{2,1,0:T(8,128)(2,1)S(1)}, bf16[2,216,128]{2,1,0:T(8,128)(2,1)S(1)}, u32[]{:S(2)}, u32[]{:S(2)}) collective-permute-start(bf16[2,216,128]{2,1,0:T(8,128)(2,1)S(1)} %fusion.28), channel_id=1, source_target_pairs={{0,8},{4,12},{8,0},{12,4},{16,24},{20,28},{24,16},{28,20},{1,9},{5... | collective-permute-start | bytes 331784 | tf_op jit(solution)/shard_map/ppermute | solution.py:40
  146.0 1.9 %collective-permute-start.10 = (bf16[216,128]{1,0:T(8,128)(2,1)S(1)}, bf16[216,128]{1,0:T(8,128)(2,1)S(1)}, u32[]{:S(2)}, u32[]{:S(2)}) collective-permute-start(bf16[216,128]{1,0:T(8,128)(2,1)S(1)} %fusion.36), channel_id=1, source_target_pairs={{0,16},{4,20},{8,24},{12,28},{16,0},{20,4},{24,8},{28,12},{1,17},{... | collective-permute-start | bytes 165896 | tf_op jit(solution)/shard_map/ppermute | solution.py:40
  148.1 2.7 %collective-permute-start.14 = (bf16[216,128]{1,0:T(8,128)(2,1)S(1)}, bf16[216,128]{1,0:T(8,128)(2,1)S(1)}, u32[]{:S(2)}, u32[]{:S(2)}) collective-permute-start(bf16[216,128]{1,0:T(8,128)(2,1)S(1)} %fusion.37), channel_id=1, source_target_pairs={{0,16},{4,20},{8,24},{12,28},{16,0},{20,4},{24,8},{28,12},{1,17},{... | collective-permute-start | bytes 165896 | tf_op jit(solution)/shard_map/ppermute | solution.py:40
  (131 shorter events, 33.5 us)
Async XLA Ops:
  5.0 13.7 %copy-start.12 = (s32[1,1,704]{2,1,0:T(1,128)S(1)}, s32[1,1,704]{2,1,0:T(1,128)}, u32[]{:S(2)}) copy-start(s32[1,1,704]{2,1,0:T(1,128)} %param.16) | copy-start | bytes 8452
  5.8 15.5 %all-to-all-start = ((f32[32,4,256]{2,1,0:T(4,128)}), f32[32,4,256]{2,1,0:T(4,128)S(1)}, u32[]{:S(2)}, u32[]{:S(2)}) async-start(f32[32,4,256]{2,1,0:T(4,128)} %broadcast_in_dim.116), calls=%async_computation | async-start | bytes 262144 | tf_op jit(solution)/shard_map/all_to_all | solution.py:26
  13.1 8.3 %copy-start.2 = (bf16[1,1,2048,256]{3,2,1,0:T(8,128)(2,1)S(1)}, bf16[1,1,2048,256]{3,2,1,0:T(8,128)(2,1)}, u32[]{:S(2)}) copy-start(bf16[1,1,2048,256]{3,2,1,0:T(8,128)(2,1)} %param.10) | copy-start | bytes 3145732
  13.1 8.3 %copy-start.7 = (bf16[1,1,2048,256]{3,2,1,0:T(8,128)(2,1)S(1)}, bf16[1,1,2048,256]{3,2,1,0:T(8,128)(2,1)}, u32[]{:S(2)}) copy-start(bf16[1,1,2048,256]{3,2,1,0:T(8,128)(2,1)} %param.11) | copy-start | bytes 3145732
  13.1 8.3 %copy-start.13 = (f32[256]{0:T(256)S(1)}, f32[256]{0:T(256)}, u32[]{:S(2)}) copy-start(f32[256]{0:T(256)} %param.13) | copy-start | bytes 3076
  24.5 12.2 %all-to-all-start.1 = ((f32[32,2,256]{2,1,0:T(2,128)}), f32[32,2,256]{2,1,0:T(2,128)S(1)}, u32[]{:S(2)}, u32[]{:S(2)}) async-start(f32[32,2,256]{2,1,0:T(2,128)} %broadcast_in_dim.117), calls=%async_computation.1 | async-start | bytes 131072 | tf_op jit(solution)/shard_map/all_to_all | solution.py:26
  42.1 16.1 %copy-start.4 = (bf16[704,256]{1,0:T(8,128)(2,1)}, bf16[704,256]{1,0:T(8,128)(2,1)S(1)}, u32[]{:S(2)}) copy-start(bf16[704,256]{1,0:T(8,128)(2,1)S(1)} %gather_fusion.1) | copy-start | bytes 1081348
  42.2 14.7 %copy-start.5 = (bf16[1,1,2048,256]{3,2,1,0:T(8,128)(2,1)S(1)}, bf16[1,1,2048,256]{3,2,1,0:T(8,128)(2,1)}, u32[]{:S(2)}) copy-start(bf16[1,1,2048,256]{3,2,1,0:T(8,128)(2,1)} %param.9) | copy-start | bytes 3145732
  42.2 10.5 %collective-permute-start.2 = (bf16[352,256]{1,0:T(8,128)(2,1)S(1)}, bf16[352,256]{1,0:T(8,128)(2,1)S(1)}, u32[]{:S(2)}, u32[]{:S(2)}) collective-permute-start(bf16[352,256]{1,0:T(8,128)(2,1)S(1)} %get-tuple-element.39), channel_id=1, source_target_pairs={{0,4},{4,8},{8,12},{12,16},{16,20},{20,24},{24,28},{1,5},{5,9},{9,... | collective-permute-start | bytes 540680 | tf_op jit(solution)/shard_map/ppermute | solution.py:33
  44.9 8.1 %collective-permute-start.3 = (bf16[352,256]{1,0:T(8,128)(2,1)S(1)}, bf16[352,256]{1,0:T(8,128)(2,1)S(1)}, u32[]{:S(2)}, u32[]{:S(2)}) collective-permute-start(bf16[352,256]{1,0:T(8,128)(2,1)S(1)} %get-tuple-element.40), channel_id=1, source_target_pairs={{4,0},{8,4},{12,8},{16,12},{20,16},{24,20},{28,24},{5,1},{9,5},{13... | collective-permute-start | bytes 540680 | tf_op jit(solution)/shard_map/ppermute | solution.py:33
  46.9 14.0 %collective-permute-start = (bf16[704,256]{1,0:T(8,128)(2,1)S(1)}, bf16[704,256]{1,0:T(8,128)(2,1)}, u32[]{:S(2)}, u32[]{:S(2)}) collective-permute-start(bf16[704,256]{1,0:T(8,128)(2,1)S(1)} %gather_fusion.1), channel_id=1, source_target_pairs={{0,1},{1,2},{2,3},{4,5},{5,6},{6,7},{8,9},{9,10},{10,11},{12,13},{... | collective-permute-start | bytes 1081352 | tf_op jit(solution)/shard_map/ppermute | solution.py:33
  49.3 11.6 %collective-permute-start.1 = (bf16[704,256]{1,0:T(8,128)(2,1)S(1)}, bf16[704,256]{1,0:T(8,128)(2,1)S(1)}, u32[]{:S(2)}, u32[]{:S(2)}) collective-permute-start(bf16[704,256]{1,0:T(8,128)(2,1)S(1)} %gather_fusion.1), channel_id=1, source_target_pairs={{1,0},{2,1},{3,2},{5,4},{6,5},{7,6},{9,8},{10,9},{11,10},{13,12},{... | collective-permute-start | bytes 1081352 | tf_op jit(solution)/shard_map/ppermute | solution.py:33
  53.0 7.9 %collective-permute-start.4 = (bf16[2,352,256]{2,1,0:T(8,128)(2,1)S(1)}, bf16[2,352,256]{2,1,0:T(8,128)(2,1)S(1)}, u32[]{:S(2)}, u32[]{:S(2)}) collective-permute-start(bf16[2,352,256]{2,1,0:T(8,128)(2,1)S(1)} %pad_maximum_fusion.pair_ref), channel_id=1, source_target_pairs={{0,1},{1,2},{2,3},{4,5},{5,6},{6,7},{8,9},{9,10},{10,11},{12,13},{... | collective-permute-start | bytes 1081352 | tf_op jit(solution)/shard_map/ppermute | solution.py:33
  54.3 6.6 %collective-permute-start.5 = (bf16[2,352,256]{2,1,0:T(8,128)(2,1)S(1)}, bf16[2,352,256]{2,1,0:T(8,128)(2,1)}, u32[]{:S(2)}, u32[]{:S(2)}) collective-permute-start(bf16[2,352,256]{2,1,0:T(8,128)(2,1)S(1)} %pad_maximum_fusion.pair_ref), channel_id=1, source_target_pairs={{1,0},{2,1},{3,2},{5,4},{6,5},{7,6},{9,8},{10,9},{11,10},{13,12},{... | collective-permute-start | bytes 1081352 | tf_op jit(solution)/shard_map/ppermute | solution.py:33
  99.8 13.9 %collective-permute-start.6 = (bf16[2,2,2,2,216,256]{5,4,0,1,3,2:T(8,128)(2,1)}, bf16[2,2,2,2,216,256]{5,4,0,1,3,2:T(8,128)(2,1)}, u32[]{:S(2)}, u32[]{:S(2)}) collective-permute-start(bf16[2,2,2,2,216,256]{5,4,0,1,3,2:T(8,128)(2,1)} %fusion.21), channel_id=1, source_target_pairs={{0,1},{1,0},{2,3},{3,2},{4,5},{5,4},{6,7},{7,6},{8,9},{9,8},{10,11... | collective-permute-start | bytes 5308424 | tf_op jit(solution)/shard_map/ppermute | solution.py:40
  102.6 11.1 %copy-start.3 = (f32[6912,256]{1,0:T(8,128)S(1)}, f32[6912,256]{1,0:T(8,128)}, u32[]{:S(2)}) copy-start(f32[6912,256]{1,0:T(8,128)} %get-tuple-element.7) | copy-start | bytes 21233668
  116.0 12.6 %collective-permute-start.7 = (bf16[2,2,2,216,128]{4,3,0,1,2:T(8,128)(2,1)S(1)}, bf16[2,2,2,216,128]{4,3,0,1,2:T(8,128)(2,1)S(1)}, u32[]{:S(2)}, u32[]{:S(2)}) collective-permute-start(bf16[2,2,2,216,128]{4,3,0,1,2:T(8,128)(2,1)S(1)} %fusion.23), channel_id=1, source_target_pairs={{0,2},{1,3},{2,0},{3,1},{4,6},{5,7},{6,4},{7,5},{8,10},{9,11},{10,... | collective-permute-start | bytes 1327112 | tf_op jit(solution)/shard_map/ppermute | solution.py:40
  122.1 13.1 %collective-permute-start.11 = (bf16[2,2,2,216,128]{4,3,0,1,2:T(8,128)(2,1)S(1)}, bf16[2,2,2,216,128]{4,3,0,1,2:T(8,128)(2,1)S(1)}, u32[]{:S(2)}, u32[]{:S(2)}) collective-permute-start(bf16[2,2,2,216,128]{4,3,0,1,2:T(8,128)(2,1)S(1)} %fusion.24), channel_id=1, source_target_pairs={{0,4},{4,0},{8,12},{12,8},{16,20},{20,16},{24,28},{28,24},{1,5},{5... | collective-permute-start | bytes 1327112 | tf_op jit(solution)/shard_map/ppermute | solution.py:40
  128.7 10.4 %collective-permute-start.8 = (bf16[2,2,216,128]{3,2,0,1:T(8,128)(2,1)S(1)}, bf16[2,2,216,128]{3,2,0,1:T(8,128)(2,1)S(1)}, u32[]{:S(2)}, u32[]{:S(2)}) collective-permute-start(bf16[2,2,216,128]{3,2,0,1:T(8,128)(2,1)S(1)} %fusion.25), channel_id=1, source_target_pairs={{0,4},{4,0},{8,12},{12,8},{16,20},{20,16},{24,28},{28,24},{1,5},{5... | collective-permute-start | bytes 663560 | tf_op jit(solution)/shard_map/ppermute | solution.py:40
  135.3 7.0 %collective-permute-start.12 = (bf16[2,2,216,128]{3,2,0,1:T(8,128)(2,1)S(1)}, bf16[2,2,216,128]{3,2,0,1:T(8,128)(2,1)S(1)}, u32[]{:S(2)}, u32[]{:S(2)}) collective-permute-start(bf16[2,2,216,128]{3,2,0,1:T(8,128)(2,1)S(1)} %fusion.26), channel_id=1, source_target_pairs={{0,2},{1,3},{2,0},{3,1},{4,6},{5,7},{6,4},{7,5},{8,10},{9,11},{10,... | collective-permute-start | bytes 663560 | tf_op jit(solution)/shard_map/ppermute | solution.py:40
  139.3 6.7 %collective-permute-start.9 = (bf16[2,216,128]{2,1,0:T(8,128)(2,1)S(1)}, bf16[2,216,128]{2,1,0:T(8,128)(2,1)S(1)}, u32[]{:S(2)}, u32[]{:S(2)}) collective-permute-start(bf16[2,216,128]{2,1,0:T(8,128)(2,1)S(1)} %fusion.27), channel_id=1, source_target_pairs={{0,8},{4,12},{8,0},{12,4},{16,24},{20,28},{24,16},{28,20},{1,9},{5... | collective-permute-start | bytes 331784 | tf_op jit(solution)/shard_map/ppermute | solution.py:40
  142.4 5.6 %collective-permute-start.13 = (bf16[2,216,128]{2,1,0:T(8,128)(2,1)S(1)}, bf16[2,216,128]{2,1,0:T(8,128)(2,1)S(1)}, u32[]{:S(2)}, u32[]{:S(2)}) collective-permute-start(bf16[2,216,128]{2,1,0:T(8,128)(2,1)S(1)} %fusion.28), channel_id=1, source_target_pairs={{0,8},{4,12},{8,0},{12,4},{16,24},{20,28},{24,16},{28,20},{1,9},{5... | collective-permute-start | bytes 331784 | tf_op jit(solution)/shard_map/ppermute | solution.py:40
  146.0 5.9 %collective-permute-start.10 = (bf16[216,128]{1,0:T(8,128)(2,1)S(1)}, bf16[216,128]{1,0:T(8,128)(2,1)S(1)}, u32[]{:S(2)}, u32[]{:S(2)}) collective-permute-start(bf16[216,128]{1,0:T(8,128)(2,1)S(1)} %fusion.36), channel_id=1, source_target_pairs={{0,16},{4,20},{8,24},{12,28},{16,0},{20,4},{24,8},{28,12},{1,17},{... | collective-permute-start | bytes 165896 | tf_op jit(solution)/shard_map/ppermute | solution.py:40
  148.1 5.1 %collective-permute-start.14 = (bf16[216,128]{1,0:T(8,128)(2,1)S(1)}, bf16[216,128]{1,0:T(8,128)(2,1)S(1)}, u32[]{:S(2)}, u32[]{:S(2)}) collective-permute-start(bf16[216,128]{1,0:T(8,128)(2,1)S(1)} %fusion.37), channel_id=1, source_target_pairs={{0,16},{4,20},{8,24},{12,28},{16,0},{20,4},{24,8},{28,12},{1,17},{... | collective-permute-start | bytes 165896 | tf_op jit(solution)/shard_map/ppermute | solution.py:40
  (11 other events, 53.7 us)
